TPU v7x, 256 devices: a whole 4x4x8 slice. The times are simulated.
256 devices in a mesh: ctx: 128 (over z, x, y), rep: 2 (over core).
Axes of the slice: x: 4, y: 4, z: 8, core: 2. Of those that a mesh axis runs over, the one named last changes fastest.
Arguments:
- queries: bfloat16 [32768, 2048], P(('rep', 'ctx')), parts along dimension 0, may hold values from -32 to 32
- encoded_key_heads: bfloat16 [32768, 256], P(('rep', 'ctx')), parts along dimension 0, may hold values from -6 to 6
- value_head_vectors: bfloat16 [32768, 256], P(('rep', 'ctx')), parts along dimension 0, may hold values from -6 to 6
- residual: bfloat16 [32768, 2048], P(('rep', 'ctx')), parts along dimension 0, may hold values from -3 to 3
- out_matrix: bfloat16 [2048, 2048], P('ctx'), may hold values from -0.125 to 0.125
- norm_gain: float32 [2048], replicated, may hold values from 0.5 to 1.5
- expert_ids: int32 [32768, 8], P(('rep', 'ctx')), parts along dimension 0, may hold values from 0 to 127, all different within a row; in each aligned block of 128 rows (0 to 127, 128 to 255, ...) at most 9 rows name the same one
- expert_gates: float32 [32768, 8], P(('rep', 'ctx')), parts along dimension 0, may hold values from 0.02 to 0.5
- gate_matrix: bfloat16 [128, 2048, 768], P('ctx'), may hold values from -0.125 to 0.125
- lift_matrix: bfloat16 [128, 2048, 768], P('ctx'), may hold values from -0.125 to 0.125
- down_matrix: bfloat16 [128, 768, 2048], P('ctx'), may hold values from -0.21875 to 0.21875
- block_mask: int32 [64, 32], P('rep'), parts along dimension 0, may hold values from 0 to 1, as said below
Outputs:
- layer_out: bfloat16 [32768, 2048], P(('rep', 'ctx')), parts along dimension 0
There are 2 independent parts, one for each index of `rep`. A program takes and returns all parts, laid end to end along the dimension named above; an argument that names none is the same for every part. Nothing has to cross between parts.
Inputs may be any that keep to these rules, and one draw needn't show every extreme that they name: block_mask[i, j] is 1 exactly when blocks i and j belong to the same document and j <= i; a document is a run of 1 to 4 blocks, and one document has 4 blocks. `expert_ids`: each token names 8 different experts. Among the 128 tokens of one index of ctx no expert is named more than 9 times, a bound that some block reaches.
All inputs are finite; a program needn't handle non-finite values.
Results may differ from a plain program's by a relative error of at most 0.015.
Values may be sent and summed in bfloat16 or wider, within the bound.
A program may use at most 128 MiB of HBM per device.

v0:
```python
import math

import jax
import jax.numpy as jnp
from jax import lax
from jax.sharding import PartitionSpec as P

QUERY_HEADS = 16
KEY_VALUE_HEADS = 2
HEAD_SIZE = 128
TOP = 8
MASK_BLOCK_SIZE = 512
DOCUMENT_BLOCKS = 4


def shifted(value, axis, steps):
    count = lax.axis_size(axis)
    initial, last = (max(0, -steps), min(count, count - steps))
    return lax.ppermute(value, axis, [(source, source + steps) for source in range(initial, last)])


def attend(queries, document_window, block_mask, block_extent):
    total_row_count = queries.shape[0]
    group_total = QUERY_HEADS // KEY_VALUE_HEADS
    device = lax.axis_index("ctx")
    per_block = MASK_BLOCK_SIZE // total_row_count
    query_block = device // per_block
    shard_device = device - (block_extent - 1) + jnp.arange(block_extent, dtype=jnp.int32)
    shard_block = jnp.maximum(shard_device, 0) // per_block
    mask_row = lax.dynamic_index_in_dim(block_mask, query_block, 0, keepdims=False)
    block_ids = jnp.arange(block_mask.shape[1], dtype=jnp.int32)
    lookup = jnp.sum(
        jnp.where(shard_block[:, None] == block_ids[None, :], mask_row[None, :], 0), axis=1
    )
    shard_open = (shard_device >= 0) & (lookup == 1)
    flat = jnp.arange(block_extent * total_row_count, dtype=jnp.int32)
    shard_of = flat // total_row_count
    place_of = flat % total_row_count
    open_key = jnp.take(shard_open, shard_of)
    query_place = jnp.arange(total_row_count, dtype=jnp.int32)
    visible = open_key[None, :] & (
        (shard_of[None, :] < block_extent - 1) | (place_of[None, :] <= query_place[:, None])
    )
    key_flattened = document_window[:, 0].reshape(
        block_extent * total_row_count, KEY_VALUE_HEADS, HEAD_SIZE
    )
    value_flattened = document_window[:, 1].reshape(
        block_extent * total_row_count, KEY_VALUE_HEADS, HEAD_SIZE
    )
    query_partition = queries.reshape(total_row_count, KEY_VALUE_HEADS, group_total, HEAD_SIZE)
    outputs = []
    for group_of_head in range(KEY_VALUE_HEADS):
        scores = jnp.einsum(
            "tgd,kd->gtk",
            query_partition[:, group_of_head],
            key_flattened[:, group_of_head],
            preferred_element_type=jnp.float32,
        ) / math.sqrt(HEAD_SIZE)
        scores = jnp.where(visible[None], scores, -jnp.inf)
        peak = jnp.max(scores, axis=-1, keepdims=True)
        weights = jnp.exp(scores - peak)
        probabilities = (weights / jnp.sum(weights, axis=-1, keepdims=True)).astype(jnp.bfloat16)
        blended = jnp.einsum(
            "gtk,kd->tgd",
            probabilities,
            value_flattened[:, group_of_head],
            preferred_element_type=jnp.float32,
        )
        outputs.append(blended.astype(jnp.bfloat16))
    return jnp.stack(outputs, axis=1).reshape(total_row_count, QUERY_HEADS * HEAD_SIZE)


def shards(
    queries,
    encoded_key_heads,
    value_head_vectors,
    residual,
    out_matrix,
    norm_gain,
    expert_ids,
    expert_gates,
    gate_matrix,
    lift_matrix,
    down_matrix,
    block_mask,
):
    total_row_count = queries.shape[0]
    devices = lax.axis_size("ctx")
    block_extent = DOCUMENT_BLOCKS * MASK_BLOCK_SIZE // total_row_count
    model_width = out_matrix.shape[1]
    paired = jnp.stack([encoded_key_heads, value_head_vectors])
    earlier = [shifted(paired, "ctx", distance) for distance in range(block_extent - 1, 0, -1)]
    document_window = jnp.stack(earlier + [paired])
    attended = attend(queries, document_window, block_mask, block_extent)
    projected = jnp.dot(
        attended,
        lax.all_gather(out_matrix, "ctx", axis=0, tiled=True),
        preferred_element_type=jnp.float32,
    )
    hidden_state = (residual.astype(jnp.float32) + projected).astype(jnp.bfloat16)
    widened = hidden_state.astype(jnp.float32)
    normed = (
        widened * lax.rsqrt(jnp.mean(widened * widened, axis=-1, keepdims=True) + 1e-06) * norm_gain
    ).astype(jnp.bfloat16)
    local_experts = gate_matrix.shape[0]
    experts_all = devices * local_experts
    capacity = total_row_count * TOP // experts_all + total_row_count * TOP // (8 * experts_all)
    chosen = expert_ids[:, :, None] == jnp.arange(experts_all, dtype=jnp.int32)[None, None, :]
    counts = jnp.sum(chosen.astype(jnp.int32), axis=1)
    before = jnp.cumsum(counts, axis=0) - counts
    slot_index = jnp.sum(jnp.where(chosen, before[:, None, :], 0), axis=2)
    flat_ids = expert_ids.reshape(-1)
    flat_slots = slot_index.reshape(-1)
    copies = jnp.repeat(normed, TOP, axis=0)
    outbox = (
        jnp.zeros((experts_all, capacity, model_width), jnp.bfloat16)
        .at[flat_ids, flat_slots]
        .set(copies)
    )
    outbox = outbox.reshape(devices, local_experts, capacity, model_width)
    arrived = lax.all_to_all(outbox, "ctx", split_axis=0, concat_axis=0, tiled=True)
    gate_act = jnp.einsum(
        "secd,edf->secf", arrived, gate_matrix, preferred_element_type=jnp.float32
    )
    lift_act = jnp.einsum(
        "secd,edf->secf", arrived, lift_matrix, preferred_element_type=jnp.float32
    )
    activated = (jax.nn.silu(gate_act) * lift_act).astype(jnp.bfloat16)
    produced = jnp.einsum(
        "secf,efd->secd", activated, down_matrix, preferred_element_type=jnp.float32
    ).astype(jnp.bfloat16)
    inbox = lax.all_to_all(produced, "ctx", split_axis=0, concat_axis=0, tiled=True)
    inbox = inbox.reshape(experts_all, capacity, model_width)
    fetched = inbox[flat_ids, flat_slots].reshape(total_row_count, TOP, model_width)
    combined = widened
    for column in range(TOP):
        combined = combined + expert_gates[:, column][:, None] * fetched[:, column].astype(
            jnp.float32
        )
    return combined.astype(jnp.bfloat16)


def solution(mesh):
    placed = (
        P(("rep", "ctx"), None),
        P(("rep", "ctx"), None),
        P(("rep", "ctx"), None),
        P(("rep", "ctx"), None),
        P("ctx", None),
        P(),
        P(("rep", "ctx"), None),
        P(("rep", "ctx"), None),
        P("ctx", None, None),
        P("ctx", None, None),
        P("ctx", None, None),
        P("rep", None),
    )
    return jax.shard_map(
        shards, mesh=mesh, in_specs=placed, out_specs=P(("rep", "ctx"), None), check_vma=False
    )
```

profile of v0, /device:TPU:8, one launch (start us, length us, event | category | flops | bytes accessed | tf_op | source)
XLA Modules:
  0.0 651.7 jit_solution(7771166940625588784)
XLA Ops:
  13.2 6.7 %collective-permute-start.1 = (bf16[2,128,256]{2,1,0:T(8,128)(2,1)}, bf16[2,128,256]{2,1,0:T(8,128)(2,1)}, u32[]{:S(2)}, u32[]{:S(2)}) collective-permute-start(bf16[2,128,256]{2,1,0:T(8,128)(2,1)} %pad_maximum_fusion.1), channel_id=1, source_target_pairs={{0,28},{2,30},{4,32},{6,34},{8,36},{10,38},{12,40},{14,42},{16,44}... | collective-permute-start | bytes 393224 | tf_op jit(solution)/shard_map/ppermute | solution.py:19
  20.0 5.4 collective-permute-start.2
  29.2 4.6 collective-permute-start.4
  41.6 4.5 select_reduce_fusion.1
  47.7 5.6 fusion.63
  60.4 4.8 collective-permute-start.6
  66.1 5.9 collective-permute-start.7
  80.9 6.2 collective-permute-start.10
  95.7 4.9 collective-permute-start.14
  125.1 7.1 %fusion.79 = (f32[8,128]{1,0:T(8,128)S(1)}, f32[8,128,2048]{1,2,0:T(8,128)}) fusion(pred[128,2048]{0,1:T(8,128)(4,1)S(1)} %fusion.47, bf16[128,2,8,128]{0,3,2,1:T(8,128)(2,1)} %bitcast.277, bf16[2048,1,128]{2,1,0:T(2,128)(2,1)} %get-tuple-element.17), kind=kOutput, calls=%fused_computation.176 | convolution fusion | flops 545261568 | bytes 9965568 | tf_op jit(solution)/shard_map/sub | solution.py:61
  132.2 7.1 %fusion.78 = (f32[8,128]{1,0:T(8,128)S(1)}, f32[8,128,2048]{1,2,0:T(8,128)}) fusion(pred[128,2048]{0,1:T(8,128)(4,1)S(1)} %fusion.47, bf16[128,2,8,128]{0,3,2,1:T(8,128)(2,1)} %bitcast.278, bf16[2048,1,128]{2,1,0:T(2,128)(2,1)} %get-tuple-element.18), kind=kOutput, calls=%fused_computation.175 | convolution fusion | flops 545261568 | bytes 9965568 | tf_op jit(solution)/shard_map/sub | solution.py:61
  147.1 4.9 multiply_reduce_fusion
  154.0 10.3 %scatter_custom_fusion = bf16[1152,2048]{1,0:T(8,128)(2,1)} fusion(s32[1024]{0:T(1024)S(1)} %broadcast_select_fusion, bf16[]{:T(256)} %constant.112.clone.1, bf16[128,2048]{1,0:T(8,128)(2,1)} %multiply_convert_fusion), kind=kCustom, calls=%fused_computation.18 | custom fusion | bytes 5242882
  164.3 5.4 copy.92
  169.7 192.3 %all_to_all.10 = bf16[128,1,9,2048]{3,2,1,0:T(8,128)(2,1)S(1)} all-to-all(bf16[128,1,9,2048]{3,2,1,0:T(8,128)(2,1)S(1)} %copy.92), channel_id=1, replica_groups=mesh['ctx'=128,'rep'=2] {'ctx'}, dimensions={0} | all-to-all | bytes 9437184 | tf_op jit(solution)/shard_map/all_to_all | solution.py:121
  362.0 9.1 %fusion.4 = f32[128,9,768]{2,0,1:T(8,128)S(1)} fusion(bf16[1,2048,768]{2,1,0:T(8,128)(2,1)S(1)} %copy-done.8, bf16[128,1,9,2048]{3,2,1,0:T(8,128)(2,1)S(1)} %all_to_all.10), kind=kOutput, calls=%fused_computation.12 | convolution fusion | flops 3623878656 | bytes 11403264 | tf_op jit(solution)/shard_map/secd,edf->secf/dot_general | solution.py:125
  371.1 9.3 %fusion.6 = f32[128,9,768]{2,0,1:T(8,128)S(1)} fusion(bf16[1,2048,768]{2,1,0:T(8,128)(2,1)S(1)} %copy-done.9, bf16[128,1,9,2048]{3,2,1,0:T(8,128)(2,1)S(1)} %all_to_all.10), kind=kOutput, calls=%fused_computation.14 | convolution fusion | flops 3623878656 | bytes 11403264 | tf_op jit(solution)/shard_map/secd,edf->secf/dot_general | solution.py:122
  384.7 6.3 copy.94
  391.0 10.2 %all-to-all-start.1 = ((bf16[128,1,9,2048]{3,2,1,0:T(8,128)(2,1)}), bf16[128,1,9,2048]{3,2,1,0:T(8,128)(2,1)}, u32[]{:S(2)}, u32[]{:S(2)}) async-start(bf16[128,1,9,2048]{3,2,1,0:T(8,128)(2,1)} %copy.94), calls=%async_computation.1 | async-start | bytes 16777216 | tf_op jit(solution)/shard_map/all_to_all | solution.py:132
  401.2 183.2 %all-to-all-done.1 = bf16[128,1,9,2048]{3,2,1,0:T(8,128)(2,1)} async-done(((bf16[128,1,9,2048]{3,2,1,0:T(8,128)(2,1)}), bf16[128,1,9,2048]{3,2,1,0:T(8,128)(2,1)}, u32[]{:S(2)}, u32[]{:S(2)}) %all-to-all-start.1) | async-done | bytes 4718624 | tf_op jit(solution)/shard_map/all_to_all | solution.py:132
  584.4 8.4 %copy.175 = bf16[128,1,9,2048]{3,0,2,1:T(8,128)(2,1)} copy(bf16[128,1,9,2048]{3,2,1,0:T(8,128)(2,1)} %all-to-all-done.1) | data formatting | bytes 9437184 | tf_op jit(solution)/shard_map/all_to_all | solution.py:132
  592.8 25.4 %gather_fusion = bf16[1024,2048]{1,0:T(8,128)(2,1)} fusion(bf16[128,9,2048]{2,0,1:T(8,128)(2,1)} %bitcast.272, s32[1024]{0:T(1024)S(1)} %bitcast.273), kind=kCustom, calls=%fused_computation | custom fusion | bytes 8396800 | tf_op jit(solution)/shard_map/gather | solution.py:134
  618.2 21.0 %fusion.73 = (bf16[128,1,2048]{2,1,0:T(2,128)(2,1)S(1)}, bf16[128,1,2048]{2,1,0:T(2,128)(2,1)S(1)}, bf16[128,1,2048]{2,1,0:T(2,128)(2,1)S(1)}, bf16[128,1,2048]{...) fusion(bf16[128,8,2048]{2,1,0:T(8,128)(2,1)} %bitcast.274), kind=kLoop, calls=%fused_computation.170 | loop fusion | bytes 8388608 | tf_op jit(solution)/shard_map/slice | solution.py:137
  639.2 5.5 fusion.38
  (107 shorter events, 83.4 us)
Async XLA Ops:
  6.5 373.9 %copy-start = (bf16[1,768,2048]{2,1,0:T(8,128)(2,1)S(1)}, bf16[1,768,2048]{2,1,0:T(8,128)(2,1)}, u32[]{:S(2)}) copy-start(bf16[1,768,2048]{2,1,0:T(8,128)(2,1)} %param.22) | copy-start | bytes 9437188
  6.5 96.9 %copy-start.5 = (bf16[128,256]{1,0:T(8,128)(2,1)S(1)}, bf16[128,256]{1,0:T(8,128)(2,1)}, u32[]{:S(2)}) copy-start(bf16[128,256]{1,0:T(8,128)(2,1)} %param.13) | copy-start | bytes 196612
  6.5 96.9 %copy-start.4 = (bf16[128,256]{1,0:T(8,128)(2,1)S(1)}, bf16[128,256]{1,0:T(8,128)(2,1)}, u32[]{:S(2)}) copy-start(bf16[128,256]{1,0:T(8,128)(2,1)} %param.14) | copy-start | bytes 196612
  6.5 140.5 %all-gather.2.cloned.1.call-start = ((), (), s32[]{:S(2)}) async-start(), calls=%async_computation.2 | async-start | bytes 8454144 | tf_op jit(solution)/shard_map/all_gather | solution.py:97
  8.9 46.1 %collective-permute-start = (bf16[2,128,256]{2,1,0:T(8,128)(2,1)}, bf16[2,128,256]{2,1,0:T(8,128)(2,1)}, u32[]{:S(2)}, u32[]{:S(2)}) collective-permute-start(bf16[2,128,256]{2,1,0:T(8,128)(2,1)} %pad_maximum_fusion.1), channel_id=1, source_target_pairs={{0,30},{2,32},{4,34},{6,36},{8,38},{10,40},{12,42},{14,44},{16,46}... | collective-permute-start | bytes 393224 | tf_op jit(solution)/shard_map/ppermute | solution.py:19
  13.2 47.2 %collective-permute-start.1 = (bf16[2,128,256]{2,1,0:T(8,128)(2,1)}, bf16[2,128,256]{2,1,0:T(8,128)(2,1)}, u32[]{:S(2)}, u32[]{:S(2)}) collective-permute-start(bf16[2,128,256]{2,1,0:T(8,128)(2,1)} %pad_maximum_fusion.1), channel_id=1, source_target_pairs={{0,28},{2,30},{4,32},{6,34},{8,36},{10,38},{12,40},{14,42},{16,44}... | collective-permute-start | bytes 393224 | tf_op jit(solution)/shard_map/ppermute | solution.py:19
  20.0 46.2 %collective-permute-start.2 = (bf16[2,128,256]{2,1,0:T(8,128)(2,1)}, bf16[2,128,256]{2,1,0:T(8,128)(2,1)}, u32[]{:S(2)}, u32[]{:S(2)}) collective-permute-start(bf16[2,128,256]{2,1,0:T(8,128)(2,1)} %pad_maximum_fusion.1), channel_id=1, source_target_pairs={{0,26},{2,28},{4,30},{6,32},{8,34},{10,36},{12,38},{14,40},{16,42}... | collective-permute-start | bytes 393224 | tf_op jit(solution)/shard_map/ppermute | solution.py:19
  25.4 47.5 %collective-permute-start.3 = (bf16[2,128,256]{2,1,0:T(8,128)(2,1)}, bf16[2,128,256]{2,1,0:T(8,128)(2,1)}, u32[]{:S(2)}, u32[]{:S(2)}) collective-permute-start(bf16[2,128,256]{2,1,0:T(8,128)(2,1)} %pad_maximum_fusion.1), channel_id=1, source_target_pairs={{0,24},{2,26},{4,28},{6,30},{8,32},{10,34},{12,36},{14,38},{16,40}... | collective-permute-start | bytes 393224 | tf_op jit(solution)/shard_map/ppermute | solution.py:19
  29.2 46.5 %collective-permute-start.4 = (bf16[2,128,256]{2,1,0:T(8,128)(2,1)}, bf16[2,128,256]{2,1,0:T(8,128)(2,1)}, u32[]{:S(2)}, u32[]{:S(2)}) collective-permute-start(bf16[2,128,256]{2,1,0:T(8,128)(2,1)} %pad_maximum_fusion.1), channel_id=1, source_target_pairs={{0,22},{2,24},{4,26},{6,28},{8,30},{10,32},{12,34},{14,36},{16,38}... | collective-permute-start | bytes 393224 | tf_op jit(solution)/shard_map/ppermute | solution.py:19
  55.1 25.8 %collective-permute-start.5 = (bf16[2,128,256]{2,1,0:T(8,128)(2,1)}, bf16[2,128,256]{2,1,0:T(8,128)(2,1)S(1)}, u32[]{:S(2)}, u32[]{:S(2)}) collective-permute-start(bf16[2,128,256]{2,1,0:T(8,128)(2,1)} %pad_maximum_fusion.1), channel_id=1, source_target_pairs={{0,20},{2,22},{4,24},{6,26},{8,28},{10,30},{12,32},{14,34},{16,36}... | collective-permute-start | bytes 393224 | tf_op jit(solution)/shard_map/ppermute | solution.py:19
  60.4 26.7 %collective-permute-start.6 = (bf16[2,128,256]{2,1,0:T(8,128)(2,1)}, bf16[2,128,256]{2,1,0:T(8,128)(2,1)S(1)}, u32[]{:S(2)}, u32[]{:S(2)}) collective-permute-start(bf16[2,128,256]{2,1,0:T(8,128)(2,1)} %pad_maximum_fusion.1), channel_id=1, source_target_pairs={{0,18},{2,20},{4,22},{6,24},{8,26},{10,28},{12,30},{14,32},{16,34}... | collective-permute-start | bytes 393224 | tf_op jit(solution)/shard_map/ppermute | solution.py:19
  66.1 22.3 %collective-permute-start.7 = (bf16[2,128,256]{2,1,0:T(8,128)(2,1)}, bf16[2,128,256]{2,1,0:T(8,128)(2,1)S(1)}, u32[]{:S(2)}, u32[]{:S(2)}) collective-permute-start(bf16[2,128,256]{2,1,0:T(8,128)(2,1)} %pad_maximum_fusion.1), channel_id=1, source_target_pairs={{0,16},{2,18},{4,20},{6,22},{8,24},{10,26},{12,28},{14,30},{16,32}... | collective-permute-start | bytes 393224 | tf_op jit(solution)/shard_map/ppermute | solution.py:19
  72.9 18.9 %collective-permute-start.8 = (bf16[2,128,256]{2,1,0:T(8,128)(2,1)}, bf16[2,128,256]{2,1,0:T(8,128)(2,1)S(1)}, u32[]{:S(2)}, u32[]{:S(2)}) collective-permute-start(bf16[2,128,256]{2,1,0:T(8,128)(2,1)} %pad_maximum_fusion.1), channel_id=1, source_target_pairs={{0,14},{2,16},{4,18},{6,20},{8,22},{10,24},{12,26},{14,28},{16,30}... | collective-permute-start | bytes 393224 | tf_op jit(solution)/shard_map/ppermute | solution.py:19
  75.7 20.0 %collective-permute-start.9 = (bf16[2,128,256]{2,1,0:T(8,128)(2,1)}, bf16[2,128,256]{2,1,0:T(8,128)(2,1)S(1)}, u32[]{:S(2)}, u32[]{:S(2)}) collective-permute-start(bf16[2,128,256]{2,1,0:T(8,128)(2,1)} %pad_maximum_fusion.1), channel_id=1, source_target_pairs={{0,12},{2,14},{4,16},{6,18},{8,20},{10,22},{12,24},{14,26},{16,28}... | collective-permute-start | bytes 393224 | tf_op jit(solution)/shard_map/ppermute | solution.py:19
  80.9 19.8 %collective-permute-start.10 = (bf16[2,128,256]{2,1,0:T(8,128)(2,1)}, bf16[2,128,256]{2,1,0:T(8,128)(2,1)S(1)}, u32[]{:S(2)}, u32[]{:S(2)}) collective-permute-start(bf16[2,128,256]{2,1,0:T(8,128)(2,1)} %pad_maximum_fusion.1), channel_id=1, source_target_pairs={{0,10},{2,12},{4,14},{6,16},{8,18},{10,20},{12,22},{14,24},{16,26}... | collective-permute-start | bytes 393224 | tf_op jit(solution)/shard_map/ppermute | solution.py:19
  87.1 13.5 %collective-permute-start.11 = (bf16[2,128,256]{2,1,0:T(8,128)(2,1)}, bf16[2,128,256]{2,1,0:T(8,128)(2,1)S(1)}, u32[]{:S(2)}, u32[]{:S(2)}) collective-permute-start(bf16[2,128,256]{2,1,0:T(8,128)(2,1)} %pad_maximum_fusion.1), channel_id=1, source_target_pairs={{0,8},{2,10},{4,12},{6,14},{8,16},{10,18},{12,20},{14,22},{16,24},... | collective-permute-start | bytes 393224 | tf_op jit(solution)/shard_map/ppermute | solution.py:19
  88.5 12.2 %collective-permute-start.12 = (bf16[2,128,256]{2,1,0:T(8,128)(2,1)}, bf16[2,128,256]{2,1,0:T(8,128)(2,1)S(1)}, u32[]{:S(2)}, u32[]{:S(2)}) collective-permute-start(bf16[2,128,256]{2,1,0:T(8,128)(2,1)} %pad_maximum_fusion.1), channel_id=1, source_target_pairs={{0,6},{2,8},{4,10},{6,12},{8,14},{10,16},{12,18},{14,20},{16,22},{... | collective-permute-start | bytes 393224 | tf_op jit(solution)/shard_map/ppermute | solution.py:19
  91.8 8.9 %collective-permute-start.13 = (bf16[2,128,256]{2,1,0:T(8,128)(2,1)}, bf16[2,128,256]{2,1,0:T(8,128)(2,1)S(1)}, u32[]{:S(2)}, u32[]{:S(2)}) collective-permute-start(bf16[2,128,256]{2,1,0:T(8,128)(2,1)} %pad_maximum_fusion.1), channel_id=1, source_target_pairs={{0,4},{2,6},{4,8},{6,10},{8,12},{10,14},{12,16},{14,18},{16,20},{1... | collective-permute-start | bytes 393224 | tf_op jit(solution)/shard_map/ppermute | solution.py:19
  95.7 7.7 %collective-permute-start.14 = (bf16[2,128,256]{2,1,0:T(8,128)(2,1)}, bf16[2,128,256]{2,1,0:T(8,128)(2,1)S(1)}, u32[]{:S(2)}, u32[]{:S(2)}) collective-permute-start(bf16[2,128,256]{2,1,0:T(8,128)(2,1)} %pad_maximum_fusion.1), channel_id=1, source_target_pairs={{0,2},{2,4},{4,6},{6,8},{8,10},{10,12},{12,14},{14,16},{16,18},{18... | collective-permute-start | bytes 393224 | tf_op jit(solution)/shard_map/ppermute | solution.py:19
  169.7 192.3 %copy-start.8 = (bf16[1,2048,768]{2,1,0:T(8,128)(2,1)S(1)}, bf16[1,2048,768]{2,1,0:T(8,128)(2,1)}, u32[]{:S(2)}) copy-start(bf16[1,2048,768]{2,1,0:T(8,128)(2,1)} %param.21) | copy-start | bytes 9437188
  362.0 9.1 %copy-start.9 = (bf16[1,2048,768]{2,1,0:T(8,128)(2,1)S(1)}, bf16[1,2048,768]{2,1,0:T(8,128)(2,1)}, u32[]{:S(2)}) copy-start(bf16[1,2048,768]{2,1,0:T(8,128)(2,1)} %param.20) | copy-start | bytes 9437188
  391.0 10.2 %copy-start.7 = (f32[128,8]{0,1:T(8,128)S(1)}, f32[128,8]{0,1:T(8,128)}, u32[]{:S(2)}) copy-start(f32[128,8]{0,1:T(8,128)} %param.19) | copy-start | bytes 12292
  391.0 193.4 %all-to-all-start.1 = ((bf16[128,1,9,2048]{3,2,1,0:T(8,128)(2,1)}), bf16[128,1,9,2048]{3,2,1,0:T(8,128)(2,1)}, u32[]{:S(2)}, u32[]{:S(2)}) async-start(bf16[128,1,9,2048]{3,2,1,0:T(8,128)(2,1)} %copy.94), calls=%async_computation.1 | async-start | bytes 16777216 | tf_op jit(solution)/shard_map/all_to_all | solution.py:132
  618.2 21.0 %copy-start.2 = (f32[128,2048]{1,0:T(8,128)S(1)}, f32[128,2048]{1,0:T(8,128)}, u32[]{:S(2)}) copy-start(f32[128,2048]{1,0:T(8,128)} %copy-done.1) | copy-start | bytes 3145732
  (4 other events, 17.6 us)
Sparse Core Ops, SparseCore 0:
  10.8 134.1 all-gather.1
where the time goes:
time: 658 us; the launch traced here: 652 us
  blocking collectives  192 us (29%)
  waiting for transfers between devices  187 us (28%)
  local copies, waits for them, and re-layouts  110 us (17%)
  starting transfers between devices  75.8 us (12%)
  matrix products  47 us (7%)
  other arithmetic  25.7 us (4%)
  between operations  14.1 us (2%)
    all_to_all x1, blocking collectives, shards(): lax.all_to_all(outbox, 'ctx', split_axis=0, concat_axis=0, tiled=True)  192 us
    all_to_all x1, waiting for transfers between devices, shards(): lax.all_to_all(produced, 'ctx', split_axis=0, concat_axis=0, tiled=True)  183 us
    ppermute x15, starting transfers between devices, shifted(): lax.ppermute(value, axis, [(source, source + steps) for source in range(i...  65.6 us
    unnamed x42, local copies, waits for them, and re-layouts  27.5 us
    gather x1, local copies, waits for them, and re-layouts, shards(): inbox[flat_ids, flat_slots].reshape(total_row_count, TOP, model_width)  25.4 us
    slice x1, local copies, waits for them, and re-layouts, shards(): fetched[:, column].astype(jnp.float32)  21 us
    sub x2, matrix products, attend(): weights = jnp.exp(scores - peak)  14.2 us
  transfers between devices with their start and end apart: 17, of which 2 were waited for; matrix products, arithmetic and copies ran while one was open for 11% of the time, Pallas kernels for 0%

commit v1 on v0

--- a/solution.py
+++ b/solution.py
@@ -3,6 +3,8 @@
 import jax
 import jax.numpy as jnp
 from jax import lax
+from jax.experimental import pallas as pl
+from jax.experimental.pallas import tpu as pltpu
 from jax.sharding import PartitionSpec as P
 
 QUERY_HEADS = 16
@@ -11,6 +13,347 @@
 TOP = 8
 MASK_BLOCK_SIZE = 512
 DOCUMENT_BLOCKS = 4
+
+
+MESH_ID = pl.DeviceIdType.MESH
+PLANE = ((1, 0), (3, 0), (0, 1), (0, 3), (1, 1), (3, 3), (1, 3), (3, 1), (2, 0), (0, 2), (2, 1), (2, 3), (1, 2), (3, 2), (2, 2))
+CAP = 9
+NX, NY, NZ = 4, 4, 8
+NQ = NX * NY
+
+
+def moe_kernel(
+    x_ref,
+    h_ref,
+    m_ref,
+    wg_hbm,
+    wl_hbm,
+    wd_hbm,
+    o_ref,
+    wg,
+    wl,
+    wd,
+    xg,
+    meta,
+    keys,
+    gts,
+    outbox,
+    inbox,
+    ret,
+    xs,
+    act,
+    part,
+    rsend,
+    rrecv,
+    w_sem,
+    zs,
+    zr,
+    ms,
+    mr,
+    ds_,
+    dr,
+    bs,
+    br,
+    ss,
+    sr,
+):
+    f32, bf16 = jnp.float32, jnp.bfloat16
+    width = x_ref.shape[1]
+    half = x_ref.shape[0] // 2
+    me = lax.axis_index("ctx")
+    z = me // NQ
+    q = lax.rem(me, NQ)
+    qx, qy = q // NY, lax.rem(q, NY)
+
+    def zpeer(d):
+        return lax.rem(z + d, NZ) * NQ + q
+
+    def qpeer(i):
+        return lax.rem(qx + PLANE[i][0], NX) * NY + lax.rem(qy + PLANE[i][1], NY)
+
+    def remote(src, dst, s_sem, r_sem, dev):
+        return pltpu.make_async_remote_copy(
+            src_ref=src, dst_ref=dst, send_sem=s_sem, recv_sem=r_sem, device_id={"ctx": dev}, device_id_type=MESH_ID
+        )
+
+    weights = [
+        pltpu.make_async_copy(a, b, w_sem.at[i])
+        for i, (a, b) in enumerate(((wg_hbm.at[0], wg), (wl_hbm.at[0], wl), (wd_hbm.at[0], wd)))
+    ]
+    for c in weights:
+        c.start()
+
+    barrier = pltpu.get_barrier_semaphore()
+    for d in range(1, NZ):
+        pl.semaphore_signal(barrier, inc=1, device_id={"ctx": zpeer(d)}, device_id_type=MESH_ID)
+    for i in range(NQ - 1):
+        pl.semaphore_signal(barrier, inc=1, device_id={"ctx": z * NQ + qpeer(i)}, device_id_type=MESH_ID)
+    pl.semaphore_wait(barrier, NZ - 1 + NQ - 1)
+
+    slot_of = {0: 0, 1: 1, 7: 2, 2: 3, 6: 4, 3: 5, 5: 6, 4: 7}
+
+    def zcopy(d, k, h):
+        src = x_ref if k == 0 else xg.at[2 * k - 1 + d]
+        rows = pl.ds(h * half, half)
+        dst = xg.at[2 * k + 1 + d] if k < 3 else xg.at[7]
+        return remote(src.at[rows], dst.at[rows], zs.at[d, k, h], zr.at[d, k, h], zpeer(1 if d == 0 else NZ - 1))
+
+    def zparts(k):
+        return [(d, h) for h in range(2) for d in range(2) if k < 3 or d == h]
+
+    for d, h in zparts(0):
+        zcopy(d, 0, h).start()
+    mcopies = []
+    for d in range(1, NZ):
+        mcopies.append(remote(m_ref, meta.at[slot_of[d]], ms.at[d - 1], mr.at[d - 1], zpeer(d)))
+    for c in mcopies:
+        c.start()
+    meta[0] = m_ref[...]
+    xg[0] = x_ref[...]
+
+    tokens = m_ref.shape[1]
+    tri = (
+        lax.broadcasted_iota(jnp.int32, (tokens, tokens), 0) < lax.broadcasted_iota(jnp.int32, (tokens, tokens), 1)
+    ).astype(bf16)
+    expert = (lax.broadcasted_iota(jnp.int32, (NQ, tokens), 0) + z * NQ).astype(f32)
+
+    def block_keys(b):
+        rows = meta[b]
+        chosen = jnp.zeros((NQ, tokens), f32)
+        gate = jnp.zeros((NQ, tokens), f32)
+        for k in range(TOP):
+            hit = expert == rows[k : k + 1, :]
+            chosen = jnp.where(hit, 1.0, chosen)
+            gate = jnp.where(hit, rows[TOP + k : TOP + k + 1, :], gate)
+        rank = jnp.dot(chosen.astype(bf16), tri, preferred_element_type=f32)
+        keys[b] = jnp.where(chosen > 0.5, rank, -100.0)
+        gts[b] = gate
+
+    row = lax.broadcasted_iota(jnp.int32, (NQ, 8, tokens), 1)
+
+    def hits(b, first):
+        return keys[b][:, None, :] == (row + first).astype(f32)
+
+    def pick(b, first):
+        return jnp.where(hits(b, first), 1.0, 0.0).reshape(NQ * 8, tokens).astype(bf16)
+
+    def build(t, blocks):
+        mats = [pick(b, first) for b, first in blocks]
+        chunk = width // 4
+
+        def piece(c, carry):
+            cols = pl.ds(pl.multiple_of(c * chunk, chunk), chunk)
+            total = None
+            for (b, _), mat in zip(blocks, mats):
+                one = jnp.dot(mat, xg[b, :, cols], preferred_element_type=f32)
+                total = one if total is None else total + one
+            outbox[t, :, :, cols] = total.astype(bf16).reshape(NQ, 8, chunk)
+            return carry
+
+        lax.fori_loop(0, 4, piece, 0)
+        for i in range(NQ - 1):
+            p = qpeer(i)
+            remote(outbox.at[t, p], inbox.at[t, q], ds_.at[t], dr.at[t], z * NQ + p).start()
+        inbox[t, q] = outbox[t, q]
+
+    def dispatch(t):
+        if isinstance(t, int) and t == 0:
+            build(0, [(0, 0)])
+        elif isinstance(t, int) and t == 8:
+            build(8, [(7, 1)])
+        else:
+            build(t, [(t - 1, 9 - t), (t, -t)])
+
+    def wait_all(buf, sem):
+        pltpu.make_async_copy(buf, buf, sem).wait()
+
+    def mlp(first, count):
+        rows = count * NQ * 8
+
+        def take(t, carry):
+            wait_all(inbox.at[first + t, pl.ds(0, NQ - 1)], dr.at[first + t])
+            xs[pl.ds(pl.multiple_of(t * NQ * 8, NQ * 8), NQ * 8), :] = inbox[first + t].reshape(NQ * 8, width)
+            return carry
+
+        lax.fori_loop(0, count, take, 0)
+        hidden = wg.shape[1]
+        tile = 256
+
+        def up(c, carry):
+            cols = pl.ds(pl.multiple_of(c * tile, tile), tile)
+            g = jnp.dot(xs[pl.ds(0, rows), :], wg[:, cols], preferred_element_type=f32)
+            u = jnp.dot(xs[pl.ds(0, rows), :], wl[:, cols], preferred_element_type=f32)
+            act[pl.ds(0, rows), cols] = (g / (1.0 + jnp.exp(-g)) * u).astype(bf16)
+            return carry
+
+        lax.fori_loop(0, hidden // tile, up, 0)
+
+        def down(c, carry):
+            cols = pl.ds(pl.multiple_of(c * tile, tile), tile)
+            y = jnp.dot(act[pl.ds(0, rows), :], wd[:, cols], preferred_element_type=f32)
+            inbox[pl.ds(first, count), :, :, cols] = y.astype(bf16).reshape(count, NQ, 8, tile)
+            return carry
+
+        lax.fori_loop(0, width // tile, down, 0)
+
+    def give_back(t):
+        for i in range(NQ - 1):
+            p = qpeer(i)
+            remote(inbox.at[t, p], ret.at[t, q], bs.at[t], br.at[t], z * NQ + p).start()
+        ret[t, q] = inbox[t, q]
+
+    block_keys(0)
+    dispatch(0)
+    for c in mcopies:
+        c.wait()
+
+    def more_keys(b, carry):
+        block_keys(b)
+        return carry
+
+    lax.fori_loop(1, NZ, more_keys, 0)
+    groups = ((0, 3), (3, 2), (5, 2), (7, 2))
+    for k in range(4):
+        for d, h in zparts(k):
+            zcopy(d, k, h).wait_recv()
+            if k < 3 and (d, h) in zparts(k + 1):
+                zcopy(d, k + 1, h).start()
+        if k < 3:
+
+            def two(t, carry):
+                dispatch(t)
+                return carry
+
+            lax.fori_loop(2 * k + 1, 2 * k + 3, two, 0)
+        else:
+            dispatch(7)
+            dispatch(8)
+        if k == 0:
+            for c in weights:
+                c.wait()
+        else:
+            mlp(*groups[k - 1])
+    mlp(*groups[3])
+
+    def back(t, carry):
+        give_back(8 - t)
+        return carry
+
+    lax.fori_loop(0, 9, back, 0)
+
+    def wait_ret(t):
+        wait_all(ret.at[t, pl.ds(0, NQ - 1)], br.at[t])
+
+    def partial(b, slot):
+        lo = jnp.where(hits(b, -b), gts[b][:, None, :], 0.0).reshape(NQ * 8, tokens)
+        hi = jnp.where(hits(b, 8 - b), gts[b][:, None, :], 0.0).reshape(NQ * 8, tokens)
+        mat = jnp.concatenate([lo, hi], axis=0).T.astype(bf16)
+        chunk = width // 4
+
+        def piece(c, carry):
+            cols = pl.ds(pl.multiple_of(c * chunk, chunk), chunk)
+            rows = ret[b : b + 2, :, :, cols].reshape(2 * NQ * 8, chunk)
+            part[slot, :, cols] = jnp.dot(mat, rows, preferred_element_type=f32)
+            return carry
+
+        lax.fori_loop(0, 4, piece, 0)
+
+    def scopy(d, k, h):
+        rows = pl.ds(h * half, half)
+        return remote(
+            rsend.at[d, k, rows], rrecv.at[d, k, rows], ss.at[d, k, h], sr.at[d, k, h], zpeer(1 if d == 0 else NZ - 1)
+        )
+
+    def sparts(k):
+        return [(d, h) for h in range(2) for d in range(2) if k > 0 or d == h]
+
+    wait_ret(8)
+    wait_ret(7)
+    partial(7, 0)
+    for d, h in sparts(0):
+        rows = pl.ds(h * half, half)
+        rsend[d, 0, rows] = part[0, rows].astype(bf16)
+        scopy(d, 0, h).start()
+    for k in range(1, 4):
+        wait_ret(8 - 2 * k)
+        wait_ret(7 - 2 * k)
+        partial(8 - 2 * k, 0)
+        partial(7 - 2 * k, 1)
+        for d, h in sparts(k):
+            rows = pl.ds(h * half, half)
+            total = part[d, rows]
+            if (d, h) in sparts(k - 1):
+                scopy(d, k - 1, h).wait_recv()
+                total = total + rrecv[d, k - 1, rows].astype(f32)
+            rsend[d, k, rows] = total.astype(bf16)
+            scopy(d, k, h).start()
+    wait_ret(0)
+    partial(0, 0)
+    for h in range(2):
+        rows = pl.ds(h * half, half)
+        total = part[0, rows] + h_ref[rows, :].astype(f32)
+        for d in range(2):
+            scopy(d, 3, h).wait_recv()
+            total = total + rrecv[d, 3, rows].astype(f32)
+        o_ref[rows, :] = total.astype(bf16)
+
+    for k in range(4):
+        for d, h in zparts(k):
+            zcopy(d, k, h).wait_send()
+        for d, h in sparts(k):
+            scopy(d, k, h).wait_send()
+
+    def sent(t, carry):
+        wait_all(outbox.at[t, pl.ds(0, NQ - 1)], ds_.at[t])
+        wait_all(inbox.at[t, pl.ds(0, NQ - 1)], bs.at[t])
+        return carry
+
+    lax.fori_loop(0, 9, sent, 0)
+
+
+def moe(normed, hidden_state, meta, gate_matrix, lift_matrix, down_matrix):
+    rows, width = normed.shape
+    ff = gate_matrix.shape[2]
+    bf16, f32 = jnp.bfloat16, jnp.float32
+    vmem = pl.BlockSpec(memory_space=pltpu.VMEM)
+    hbm = pl.BlockSpec(memory_space=pl.ANY)
+    dma = pltpu.SemaphoreType.DMA
+    return pl.pallas_call(
+        moe_kernel,
+        out_shape=jax.ShapeDtypeStruct((rows, width), bf16),
+        in_specs=[vmem, vmem, vmem, hbm, hbm, hbm],
+        out_specs=vmem,
+        scratch_shapes=[
+            pltpu.VMEM((width, ff), bf16),
+            pltpu.VMEM((width, ff), bf16),
+            pltpu.VMEM((ff, width), bf16),
+            pltpu.VMEM((NZ, rows, width), bf16),
+            pltpu.VMEM((NZ, 2 * TOP, rows), f32),
+            pltpu.VMEM((NZ, NQ, rows), f32),
+            pltpu.VMEM((NZ, NQ, rows), f32),
+            pltpu.VMEM((CAP, NQ, 8, width), bf16),
+            pltpu.VMEM((CAP, NQ, 8, width), bf16),
+            pltpu.VMEM((CAP, NQ, 8, width), bf16),
+            pltpu.VMEM((3 * NQ * 8, width), bf16),
+            pltpu.VMEM((3 * NQ * 8, ff), bf16),
+            pltpu.VMEM((2, rows, width), f32),
+            pltpu.VMEM((2, 4, rows, width), bf16),
+            pltpu.VMEM((2, 4, rows, width), bf16),
+            dma((3,)),
+            dma((2, 4, 2)),
+            dma((2, 4, 2)),
+            dma((NZ - 1,)),
+            dma((NZ - 1,)),
+            dma((CAP,)),
+            dma((CAP,)),
+            dma((CAP,)),
+            dma((CAP,)),
+            dma((2, 4, 2)),
+            dma((2, 4, 2)),
+        ],
+        compiler_params=pltpu.CompilerParams(collective_id=0, has_side_effects=True, vmem_limit_bytes=60 * 1024 * 1024),
+        name="moe",
+    )(normed, hidden_state, meta, gate_matrix, lift_matrix, down_matrix)
 
 
 def shifted(value, axis, steps):
@@ -102,42 +445,8 @@
     normed = (
         widened * lax.rsqrt(jnp.mean(widened * widened, axis=-1, keepdims=True) + 1e-06) * norm_gain
     ).astype(jnp.bfloat16)
-    local_experts = gate_matrix.shape[0]
-    experts_all = devices * local_experts
-    capacity = total_row_count * TOP // experts_all + total_row_count * TOP // (8 * experts_all)
-    chosen = expert_ids[:, :, None] == jnp.arange(experts_all, dtype=jnp.int32)[None, None, :]
-    counts = jnp.sum(chosen.astype(jnp.int32), axis=1)
-    before = jnp.cumsum(counts, axis=0) - counts
-    slot_index = jnp.sum(jnp.where(chosen, before[:, None, :], 0), axis=2)
-    flat_ids = expert_ids.reshape(-1)
-    flat_slots = slot_index.reshape(-1)
-    copies = jnp.repeat(normed, TOP, axis=0)
-    outbox = (
-        jnp.zeros((experts_all, capacity, model_width), jnp.bfloat16)
-        .at[flat_ids, flat_slots]
-        .set(copies)
-    )
-    outbox = outbox.reshape(devices, local_experts, capacity, model_width)
-    arrived = lax.all_to_all(outbox, "ctx", split_axis=0, concat_axis=0, tiled=True)
-    gate_act = jnp.einsum(
-        "secd,edf->secf", arrived, gate_matrix, preferred_element_type=jnp.float32
-    )
-    lift_act = jnp.einsum(
-        "secd,edf->secf", arrived, lift_matrix, preferred_element_type=jnp.float32
-    )
-    activated = (jax.nn.silu(gate_act) * lift_act).astype(jnp.bfloat16)
-    produced = jnp.einsum(
-        "secf,efd->secd", activated, down_matrix, preferred_element_type=jnp.float32
-    ).astype(jnp.bfloat16)
-    inbox = lax.all_to_all(produced, "ctx", split_axis=0, concat_axis=0, tiled=True)
-    inbox = inbox.reshape(experts_all, capacity, model_width)
-    fetched = inbox[flat_ids, flat_slots].reshape(total_row_count, TOP, model_width)
-    combined = widened
-    for column in range(TOP):
-        combined = combined + expert_gates[:, column][:, None] * fetched[:, column].astype(
-            jnp.float32
-        )
-    return combined.astype(jnp.bfloat16)
+    meta = jnp.concatenate([expert_ids.astype(jnp.float32).T, expert_gates.T])
+    return moe(normed, hidden_state, meta, gate_matrix, lift_matrix, down_matrix)
 
 
 def solution(mesh):

time: 658 us -> 294 us (0.45)
  blocking collectives: 192 us -> 0 us
  waiting for transfers between devices: 187 us -> 25.7 us
  Pallas kernels: 0 us -> 134 us
  local copies, waits for them, and re-layouts: 110 us -> 16.8 us
  matrix products: 47 us -> 21.6 us
  starting transfers between devices: 75.8 us -> 65.2 us
  other arithmetic: 25.7 us -> 16.3 us
    all_to_all x1 -> x0, blocking collectives: 192 us -> none  [shards(): lax.all_to_all(outbox, 'ctx', split_axis=0, concat_axis=0, tiled=True)]
    all_to_all x1 -> x0, waiting for transfers between devices: 183 us -> none  [shards(): lax.all_to_all(produced, 'ctx', split_axis=0, concat_axis=0, tiled=True)]
    pallas_call x0 -> x1, Pallas kernels: none -> 134 us  [moe(): pl.pallas_call(moe_kernel, out_shape=jax.ShapeDtypeStruct((rows, width),...]
    gather x1 -> x0, local copies, waits for them, and re-layouts: 25.4 us -> none  [shards(): inbox[flat_ids, flat_slots].reshape(total_row_count, TOP, model_width)]
    dot_general x3 -> x0, matrix products: 22.6 us -> none  [the longest x1 9.35 us: shards(): jnp.einsum('secd,edf->secf', arrived, gate_matrix, preferred_element_type...]
    all_gather x1, waiting for transfers between devices: 0.01 us -> 22.2 us  [shards(): lax.all_gather(out_matrix, 'ctx', axis=0, tiled=True)]
    slice x1 -> x0, local copies, waits for them, and re-layouts: 21 us -> none  [shards(): fetched[:, column].astype(jnp.float32)]
    unnamed x42 -> x39, local copies, waits for them, and re-layouts: 27.5 us -> 11.3 us
  transfers between devices with their start and end apart: 17 -> 16, of which waited for: 2 -> 2; matrix products, arithmetic and copies ran while one was open for 11% -> 15% of each run, Pallas kernels for 0% -> 0%
where the time goes in v1:
time: 294 us; the launch traced here: 293 us
  Pallas kernels  134 us (46%)
  starting transfers between devices  65.2 us (22%)
  waiting for transfers between devices  25.7 us (9%)
  matrix products  21.6 us (7%)
  local copies, waits for them, and re-layouts  16.8 us (6%)
  other arithmetic  16.3 us (6%)
  between operations  13.9 us (5%)
    pallas_call x1, Pallas kernels, moe(): pl.pallas_call(moe_kernel, out_shape=jax.ShapeDtypeStruct((rows, width),...  134 us
    ppermute x15, starting transfers between devices, shifted(): lax.ppermute(value, axis, [(source, source + steps) for source in range(i...  65.2 us
    all_gather x1, waiting for transfers between devices, shards(): lax.all_gather(out_matrix, 'ctx', axis=0, tiled=True)  22.2 us
    sub x2, matrix products, attend(): weights = jnp.exp(scores - peak)  11.5 us
    unnamed x39, local copies, waits for them, and re-layouts  11.3 us
  transfers between devices with their start and end apart: 16, of which 2 were waited for; matrix products, arithmetic and copies ran while one was open for 15% of the time, Pallas kernels for 0%

profile of v1, /device:TPU:8, one launch (start us, length us, event | category | flops | bytes accessed | tf_op | source)
XLA Modules:
  0.0 293.2 jit_solution(4284312827956314445)
XLA Ops:
  8.1 3.7 %collective-permute-start = (bf16[2,128,256]{2,1,0:T(8,128)(2,1)S(1)}, bf16[2,128,256]{2,1,0:T(8,128)(2,1)S(1)}, u32[]{:S(2)}, u32[]{:S(2)}) collective-permute-start(bf16[2,128,256]{2,1,0:T(8,128)(2,1)S(1)} %pad_maximum_fusion.1), channel_id=1, source_target_pairs={{0,30},{2,32},{4,34},{6,36},{8,38},{10,40},{12,42},{14,44},{16,46}... | collective-permute-start | bytes 393224 | tf_op jit(solution)/shard_map/ppermute | solution.py:362
  11.9 6.7 %collective-permute-start.1 = (bf16[2,128,256]{2,1,0:T(8,128)(2,1)S(1)}, bf16[2,128,256]{2,1,0:T(8,128)(2,1)S(1)}, u32[]{:S(2)}, u32[]{:S(2)}) collective-permute-start(bf16[2,128,256]{2,1,0:T(8,128)(2,1)S(1)} %pad_maximum_fusion.1), channel_id=1, source_target_pairs={{0,28},{2,30},{4,32},{6,34},{8,36},{10,38},{12,40},{14,42},{16,44}... | collective-permute-start | bytes 393224 | tf_op jit(solution)/shard_map/ppermute | solution.py:362
  18.6 5.4 %collective-permute-start.2 = (bf16[2,128,256]{2,1,0:T(8,128)(2,1)S(1)}, bf16[2,128,256]{2,1,0:T(8,128)(2,1)S(1)}, u32[]{:S(2)}, u32[]{:S(2)}) collective-permute-start(bf16[2,128,256]{2,1,0:T(8,128)(2,1)S(1)} %pad_maximum_fusion.1), channel_id=1, source_target_pairs={{0,26},{2,28},{4,30},{6,32},{8,34},{10,36},{12,38},{14,40},{16,42}... | collective-permute-start | bytes 393224 | tf_op jit(solution)/shard_map/ppermute | solution.py:362
  24.0 3.8 %collective-permute-start.3 = (bf16[2,128,256]{2,1,0:T(8,128)(2,1)S(1)}, bf16[2,128,256]{2,1,0:T(8,128)(2,1)S(1)}, u32[]{:S(2)}, u32[]{:S(2)}) collective-permute-start(bf16[2,128,256]{2,1,0:T(8,128)(2,1)S(1)} %pad_maximum_fusion.1), channel_id=1, source_target_pairs={{0,24},{2,26},{4,28},{6,30},{8,32},{10,34},{12,36},{14,38},{16,40}... | collective-permute-start | bytes 393224 | tf_op jit(solution)/shard_map/ppermute | solution.py:362
  27.8 4.6 %collective-permute-start.4 = (bf16[2,128,256]{2,1,0:T(8,128)(2,1)S(1)}, bf16[2,128,256]{2,1,0:T(8,128)(2,1)S(1)}, u32[]{:S(2)}, u32[]{:S(2)}) collective-permute-start(bf16[2,128,256]{2,1,0:T(8,128)(2,1)S(1)} %pad_maximum_fusion.1), channel_id=1, source_target_pairs={{0,22},{2,24},{4,26},{6,28},{8,30},{10,32},{12,34},{14,36},{16,38}... | collective-permute-start | bytes 393224 | tf_op jit(solution)/shard_map/ppermute | solution.py:362
  33.8 4.4 %select_reduce_fusion = pred[2048]{0:T(1024)(128)(4,1)S(1)} fusion(pred[]{:T(512)} %bitcast.30, pred[]{:T(512)} %bitcast.31, pred[]{:T(512)} %bitcast.32, pred[]{:T(512)} %bitcast.33, pred[]{:T(512)} %bitcast.34, pred[]{:T(512)} %bitcast.36, pred[]{:T(512)} %bitcast.35), kind=kLoop, calls=%fused_computation.61 | loop fusion | flops 47104 | bytes 2055 | tf_op jit(solution)/shard_map/jit(_take)/gather | solution.py:382
  38.2 5.6 %fusion.37 = (pred[2048]{0:T(1024)(128)(4,1)S(1)}, pred[2048]{0:T(1024)(128)(4,1)S(1)}) fusion(pred[2048]{0:T(1024)(128)(4,1)S(1)} %compare_reduce_fusion, pred[2048]{0:T(1024)(128)(4,1)S(1)} %compare_reduce_fusion.1, pred[2048]{0:T(1024)(128)(4,1)S(1)} %compare_reduce_fusion.2, pred[2048]{0:T(1024)(128)(4,1)S(1)} %compare_reduce_fusion.3, ...), kind=kLoop, calls=%fused_computation.87 | loop fusion | flops 51200 | bytes 24585 | tf_op jit(solution)/shard_map/lt | solution.py:385
  49.6 5.0 %collective-permute-start.5 = (bf16[2,128,256]{2,1,0:T(8,128)(2,1)S(1)}, bf16[2,128,256]{2,1,0:T(8,128)(2,1)S(1)}, u32[]{:S(2)}, u32[]{:S(2)}) collective-permute-start(bf16[2,128,256]{2,1,0:T(8,128)(2,1)S(1)} %pad_maximum_fusion.1), channel_id=1, source_target_pairs={{0,20},{2,22},{4,24},{6,26},{8,28},{10,30},{12,32},{14,34},{16,36}... | collective-permute-start | bytes 393224 | tf_op jit(solution)/shard_map/ppermute | solution.py:362
  54.7 4.8 %collective-permute-start.6 = (bf16[2,128,256]{2,1,0:T(8,128)(2,1)S(1)}, bf16[2,128,256]{2,1,0:T(8,128)(2,1)S(1)}, u32[]{:S(2)}, u32[]{:S(2)}) collective-permute-start(bf16[2,128,256]{2,1,0:T(8,128)(2,1)S(1)} %pad_maximum_fusion.1), channel_id=1, source_target_pairs={{0,18},{2,20},{4,22},{6,24},{8,26},{10,28},{12,30},{14,32},{16,34}... | collective-permute-start | bytes 393224 | tf_op jit(solution)/shard_map/ppermute | solution.py:362
  59.5 5.8 %collective-permute-start.7 = (bf16[2,128,256]{2,1,0:T(8,128)(2,1)S(1)}, bf16[2,128,256]{2,1,0:T(8,128)(2,1)S(1)}, u32[]{:S(2)}, u32[]{:S(2)}) collective-permute-start(bf16[2,128,256]{2,1,0:T(8,128)(2,1)S(1)} %pad_maximum_fusion.1), channel_id=1, source_target_pairs={{0,16},{2,18},{4,20},{6,22},{8,24},{10,26},{12,28},{14,30},{16,32}... | collective-permute-start | bytes 393224 | tf_op jit(solution)/shard_map/ppermute | solution.py:362
  67.2 4.2 %collective-permute-start.9 = (bf16[2,128,256]{2,1,0:T(8,128)(2,1)S(1)}, bf16[2,128,256]{2,1,0:T(8,128)(2,1)S(1)}, u32[]{:S(2)}, u32[]{:S(2)}) collective-permute-start(bf16[2,128,256]{2,1,0:T(8,128)(2,1)S(1)} %pad_maximum_fusion.1), channel_id=1, source_target_pairs={{0,12},{2,14},{4,16},{6,18},{8,20},{10,22},{12,24},{14,26},{16,28}... | collective-permute-start | bytes 393224 | tf_op jit(solution)/shard_map/ppermute | solution.py:362
  71.5 6.2 %collective-permute-start.10 = (bf16[2,128,256]{2,1,0:T(8,128)(2,1)S(1)}, bf16[2,128,256]{2,1,0:T(8,128)(2,1)S(1)}, u32[]{:S(2)}, u32[]{:S(2)}) collective-permute-start(bf16[2,128,256]{2,1,0:T(8,128)(2,1)S(1)} %pad_maximum_fusion.1), channel_id=1, source_target_pairs={{0,10},{2,12},{4,14},{6,16},{8,18},{10,20},{12,22},{14,24},{16,26}... | collective-permute-start | bytes 393224 | tf_op jit(solution)/shard_map/ppermute | solution.py:362
  79.1 3.3 %collective-permute-start.12 = (bf16[2,128,256]{2,1,0:T(8,128)(2,1)S(1)}, bf16[2,128,256]{2,1,0:T(8,128)(2,1)S(1)}, u32[]{:S(2)}, u32[]{:S(2)}) collective-permute-start(bf16[2,128,256]{2,1,0:T(8,128)(2,1)S(1)} %pad_maximum_fusion.1), channel_id=1, source_target_pairs={{0,6},{2,8},{4,10},{6,12},{8,14},{10,16},{12,18},{14,20},{16,22},{... | collective-permute-start | bytes 393224 | tf_op jit(solution)/shard_map/ppermute | solution.py:362
  82.5 3.8 %collective-permute-start.13 = (bf16[2,128,256]{2,1,0:T(8,128)(2,1)S(1)}, bf16[2,128,256]{2,1,0:T(8,128)(2,1)S(1)}, u32[]{:S(2)}, u32[]{:S(2)}) collective-permute-start(bf16[2,128,256]{2,1,0:T(8,128)(2,1)S(1)} %pad_maximum_fusion.1), channel_id=1, source_target_pairs={{0,4},{2,6},{4,8},{6,10},{8,12},{10,14},{12,16},{14,18},{16,20},{1... | collective-permute-start | bytes 393224 | tf_op jit(solution)/shard_map/ppermute | solution.py:362
  86.3 4.7 %collective-permute-start.14 = (bf16[2,128,256]{2,1,0:T(8,128)(2,1)S(1)}, bf16[2,128,256]{2,1,0:T(8,128)(2,1)S(1)}, u32[]{:S(2)}, u32[]{:S(2)}) collective-permute-start(bf16[2,128,256]{2,1,0:T(8,128)(2,1)S(1)} %pad_maximum_fusion.1), channel_id=1, source_target_pairs={{0,2},{2,4},{4,6},{6,8},{8,10},{10,12},{12,14},{14,16},{16,18},{18... | collective-permute-start | bytes 393224 | tf_op jit(solution)/shard_map/ppermute | solution.py:362
  91.1 2.8 collective-permute-done.14
  94.8 2.4 fusion.47
  97.2 3.5 %copy.40 = bf16[2048,1,128]{0,2,1:T(8,128)(2,1)} copy(bf16[2048,1,128]{2,1,0:T(2,128)(2,1)} %get-tuple-element.7) | data formatting | bytes 1048576
  104.0 6.9 %fusion.51 = (f32[8,128]{1,0:T(8,128)S(1)}, f32[8,128,2048]{1,2,0:T(8,128)}) fusion(pred[128,2048]{0,1:T(8,128)(4,1)S(1)} %fusion.21, bf16[128,2,8,128]{0,3,2,1:T(8,128)(2,1)} %bitcast.150, bf16[2048,1,128]{2,1,0:T(2,128)(2,1)S(1)} %get-tuple-element.9), kind=kOutput, calls=%fused_computation.110 | convolution fusion | flops 545261568 | bytes 9441280 | tf_op jit(solution)/shard_map/sub | solution.py:404
  110.9 4.7 %fusion.50 = (f32[8,128]{1,0:T(8,128)S(1)}, f32[8,128,2048]{1,2,0:T(8,128)}) fusion(pred[128,2048]{0,1:T(8,128)(4,1)S(1)} %fusion.21, bf16[128,2,8,128]{0,3,2,1:T(8,128)(2,1)S(1)} %bitcast.151, bf16[2048,1,128]{2,1,0:T(2,128)(2,1)S(1)} %get-tuple-element.10), kind=kOutput, calls=%fused_computation.109 | convolution fusion | flops 545261568 | bytes 9965568 | tf_op jit(solution)/shard_map/sub | solution.py:404
  115.6 4.5 %fusion.15 = bf16[128,1,8,128]{0,3,2,1:T(8,128)(2,1)S(1)} fusion(f32[8,128,2048]{1,2,0:T(8,128)} %get-tuple-element.30, f32[8,128]{1,0:T(8,128)S(1)} %get-tuple-element.29, bf16[2048,1,128]{0,2,1:T(8,128)(2,1)S(1)} %copy-done.4), kind=kOutput, calls=%fused_computation.24 | convolution fusion | flops 541196288 | bytes 9179136 | tf_op jit(solution)/shard_map/gtk,kd->tgd/dot_general | solution.py:406
  122.8 22.2 %all-gather.2.cloned.1.call-done = bf16[2048,2048]{1,0:T(8,128)(2,1)} async-done(((bf16[16,2048]{1,0:T(8,128)(2,1)}), bf16[2048,2048]{1,0:T(8,128)(2,1)}) %all-gather.2.cloned.1.call-update) | async-done | bytes 8388624 | tf_op jit(solution)/shard_map/all_gather | solution.py:440
  145.0 4.8 %fusion.17 = (f32[128]{0:T(128)S(1)}, bf16[128,2048]{1,0:T(8,128)(2,1)S(1)}) fusion(bf16[128,2048]{0,1:T(8,128)(2,1)S(1)} %bitcast.149, bf16[2048,2048]{1,0:T(8,128)(2,1)} %all-gather.2.cloned.1.call-done, bf16[128,2048]{1,0:T(8,128)(2,1)S(1)} %copy-done.2), kind=kOutput, calls=%fused_computation.26 | convolution fusion | flops 1075314560 | bytes 9961984 | tf_op jit(solution)/shard_map/dot_general | solution.py:438
  150.8 133.7 %moe.1 = bf16[128,2048]{1,0:T(8,128)(2,1)} custom-call(bf16[128,2048]{1,0:T(8,128)(2,1)} %fusion.19.x_ref, bf16[128,2048]{1,0:T(8,128)(2,1)} %copy-done.1, f32[16,128]{1,0:T(8,128)} %pad_maximum_fusion.2.m_ref, bf16[1,2048,768]{2,1,0:T(8,128)(2,1)} %wg_hbm.1, bf16[1,2048,768]{2,1,0:T(8,128)(2,1)} %wl_hbm.1, bf16[1,768,2048]{2,1,0:T(8,128)(2,1)} %wd_hbm.1), custom_call_target="tpu_custom_call" | custom-call | tf_op jit(solution)/shard_map/moe/pallas_call | solution.py:321
  (84 shorter events, 21.8 us)
Async XLA Ops:
  6.5 26.3 %copy-start = (s32[32,32]{1,0:T(8,128)S(1)}, s32[32,32]{1,0:T(8,128)}, u32[]{:S(2)}) copy-start(s32[32,32]{1,0:T(8,128)} %param.23) | copy-start | bytes 12292
  6.5 138.4 %all-gather.2.cloned.1.call-start = ((), (), s32[]{:S(2)}) async-start(), calls=%async_computation | async-start | bytes 8454144 | tf_op jit(solution)/shard_map/all_gather | solution.py:440
  8.1 41.4 %collective-permute-start = (bf16[2,128,256]{2,1,0:T(8,128)(2,1)S(1)}, bf16[2,128,256]{2,1,0:T(8,128)(2,1)S(1)}, u32[]{:S(2)}, u32[]{:S(2)}) collective-permute-start(bf16[2,128,256]{2,1,0:T(8,128)(2,1)S(1)} %pad_maximum_fusion.1), channel_id=1, source_target_pairs={{0,30},{2,32},{4,34},{6,36},{8,38},{10,40},{12,42},{14,44},{16,46}... | collective-permute-start | bytes 393224 | tf_op jit(solution)/shard_map/ppermute | solution.py:362
  11.9 42.8 %collective-permute-start.1 = (bf16[2,128,256]{2,1,0:T(8,128)(2,1)S(1)}, bf16[2,128,256]{2,1,0:T(8,128)(2,1)S(1)}, u32[]{:S(2)}, u32[]{:S(2)}) collective-permute-start(bf16[2,128,256]{2,1,0:T(8,128)(2,1)S(1)} %pad_maximum_fusion.1), channel_id=1, source_target_pairs={{0,28},{2,30},{4,32},{6,34},{8,36},{10,38},{12,40},{14,42},{16,44}... | collective-permute-start | bytes 393224 | tf_op jit(solution)/shard_map/ppermute | solution.py:362
  18.6 40.9 %collective-permute-start.2 = (bf16[2,128,256]{2,1,0:T(8,128)(2,1)S(1)}, bf16[2,128,256]{2,1,0:T(8,128)(2,1)S(1)}, u32[]{:S(2)}, u32[]{:S(2)}) collective-permute-start(bf16[2,128,256]{2,1,0:T(8,128)(2,1)S(1)} %pad_maximum_fusion.1), channel_id=1, source_target_pairs={{0,26},{2,28},{4,30},{6,32},{8,34},{10,36},{12,38},{14,40},{16,42}... | collective-permute-start | bytes 393224 | tf_op jit(solution)/shard_map/ppermute | solution.py:362
  24.0 41.4 %collective-permute-start.3 = (bf16[2,128,256]{2,1,0:T(8,128)(2,1)S(1)}, bf16[2,128,256]{2,1,0:T(8,128)(2,1)S(1)}, u32[]{:S(2)}, u32[]{:S(2)}) collective-permute-start(bf16[2,128,256]{2,1,0:T(8,128)(2,1)S(1)} %pad_maximum_fusion.1), channel_id=1, source_target_pairs={{0,24},{2,26},{4,28},{6,30},{8,32},{10,34},{12,36},{14,38},{16,40}... | collective-permute-start | bytes 393224 | tf_op jit(solution)/shard_map/ppermute | solution.py:362
  27.8 39.4 %collective-permute-start.4 = (bf16[2,128,256]{2,1,0:T(8,128)(2,1)S(1)}, bf16[2,128,256]{2,1,0:T(8,128)(2,1)S(1)}, u32[]{:S(2)}, u32[]{:S(2)}) collective-permute-start(bf16[2,128,256]{2,1,0:T(8,128)(2,1)S(1)} %pad_maximum_fusion.1), channel_id=1, source_target_pairs={{0,22},{2,24},{4,26},{6,28},{8,30},{10,32},{12,34},{14,36},{16,38}... | collective-permute-start | bytes 393224 | tf_op jit(solution)/shard_map/ppermute | solution.py:362
  48.3 45.6 %copy-start.6 = (bf16[128,256]{1,0:T(8,128)(2,1)S(1)}, bf16[128,256]{1,0:T(8,128)(2,1)}, u32[]{:S(2)}) copy-start(bf16[128,256]{1,0:T(8,128)(2,1)} %param.14) | copy-start | bytes 196612
  48.3 45.6 %copy-start.7 = (bf16[128,256]{1,0:T(8,128)(2,1)S(1)}, bf16[128,256]{1,0:T(8,128)(2,1)}, u32[]{:S(2)}) copy-start(bf16[128,256]{1,0:T(8,128)(2,1)} %param.13) | copy-start | bytes 196612
  49.6 21.9 %collective-permute-start.5 = (bf16[2,128,256]{2,1,0:T(8,128)(2,1)S(1)}, bf16[2,128,256]{2,1,0:T(8,128)(2,1)S(1)}, u32[]{:S(2)}, u32[]{:S(2)}) collective-permute-start(bf16[2,128,256]{2,1,0:T(8,128)(2,1)S(1)} %pad_maximum_fusion.1), channel_id=1, source_target_pairs={{0,20},{2,22},{4,24},{6,26},{8,28},{10,30},{12,32},{14,34},{16,36}... | collective-permute-start | bytes 393224 | tf_op jit(solution)/shard_map/ppermute | solution.py:362
  54.7 23.1 %collective-permute-start.6 = (bf16[2,128,256]{2,1,0:T(8,128)(2,1)S(1)}, bf16[2,128,256]{2,1,0:T(8,128)(2,1)S(1)}, u32[]{:S(2)}, u32[]{:S(2)}) collective-permute-start(bf16[2,128,256]{2,1,0:T(8,128)(2,1)S(1)} %pad_maximum_fusion.1), channel_id=1, source_target_pairs={{0,18},{2,20},{4,22},{6,24},{8,26},{10,28},{12,30},{14,32},{16,34}... | collective-permute-start | bytes 393224 | tf_op jit(solution)/shard_map/ppermute | solution.py:362
  59.5 19.6 %collective-permute-start.7 = (bf16[2,128,256]{2,1,0:T(8,128)(2,1)S(1)}, bf16[2,128,256]{2,1,0:T(8,128)(2,1)S(1)}, u32[]{:S(2)}, u32[]{:S(2)}) collective-permute-start(bf16[2,128,256]{2,1,0:T(8,128)(2,1)S(1)} %pad_maximum_fusion.1), channel_id=1, source_target_pairs={{0,16},{2,18},{4,20},{6,22},{8,24},{10,26},{12,28},{14,30},{16,32}... | collective-permute-start | bytes 393224 | tf_op jit(solution)/shard_map/ppermute | solution.py:362
  65.4 17.1 %collective-permute-start.8 = (bf16[2,128,256]{2,1,0:T(8,128)(2,1)S(1)}, bf16[2,128,256]{2,1,0:T(8,128)(2,1)S(1)}, u32[]{:S(2)}, u32[]{:S(2)}) collective-permute-start(bf16[2,128,256]{2,1,0:T(8,128)(2,1)S(1)} %pad_maximum_fusion.1), channel_id=1, source_target_pairs={{0,14},{2,16},{4,18},{6,20},{8,22},{10,24},{12,26},{14,28},{16,30}... | collective-permute-start | bytes 393224 | tf_op jit(solution)/shard_map/ppermute | solution.py:362
  67.2 19.1 %collective-permute-start.9 = (bf16[2,128,256]{2,1,0:T(8,128)(2,1)S(1)}, bf16[2,128,256]{2,1,0:T(8,128)(2,1)S(1)}, u32[]{:S(2)}, u32[]{:S(2)}) collective-permute-start(bf16[2,128,256]{2,1,0:T(8,128)(2,1)S(1)} %pad_maximum_fusion.1), channel_id=1, source_target_pairs={{0,12},{2,14},{4,16},{6,18},{8,20},{10,22},{12,24},{14,26},{16,28}... | collective-permute-start | bytes 393224 | tf_op jit(solution)/shard_map/ppermute | solution.py:362
  71.5 19.5 %collective-permute-start.10 = (bf16[2,128,256]{2,1,0:T(8,128)(2,1)S(1)}, bf16[2,128,256]{2,1,0:T(8,128)(2,1)S(1)}, u32[]{:S(2)}, u32[]{:S(2)}) collective-permute-start(bf16[2,128,256]{2,1,0:T(8,128)(2,1)S(1)} %pad_maximum_fusion.1), channel_id=1, source_target_pairs={{0,10},{2,12},{4,14},{6,16},{8,18},{10,20},{12,22},{14,24},{16,26}... | collective-permute-start | bytes 393224 | tf_op jit(solution)/shard_map/ppermute | solution.py:362
  77.8 13.2 %collective-permute-start.11 = (bf16[2,128,256]{2,1,0:T(8,128)(2,1)S(1)}, bf16[2,128,256]{2,1,0:T(8,128)(2,1)S(1)}, u32[]{:S(2)}, u32[]{:S(2)}) collective-permute-start(bf16[2,128,256]{2,1,0:T(8,128)(2,1)S(1)} %pad_maximum_fusion.1), channel_id=1, source_target_pairs={{0,8},{2,10},{4,12},{6,14},{8,16},{10,18},{12,20},{14,22},{16,24},... | collective-permute-start | bytes 393224 | tf_op jit(solution)/shard_map/ppermute | solution.py:362
  79.1 11.9 %collective-permute-start.12 = (bf16[2,128,256]{2,1,0:T(8,128)(2,1)S(1)}, bf16[2,128,256]{2,1,0:T(8,128)(2,1)S(1)}, u32[]{:S(2)}, u32[]{:S(2)}) collective-permute-start(bf16[2,128,256]{2,1,0:T(8,128)(2,1)S(1)} %pad_maximum_fusion.1), channel_id=1, source_target_pairs={{0,6},{2,8},{4,10},{6,12},{8,14},{10,16},{12,18},{14,20},{16,22},{... | collective-permute-start | bytes 393224 | tf_op jit(solution)/shard_map/ppermute | solution.py:362
  82.5 8.6 %collective-permute-start.13 = (bf16[2,128,256]{2,1,0:T(8,128)(2,1)S(1)}, bf16[2,128,256]{2,1,0:T(8,128)(2,1)S(1)}, u32[]{:S(2)}, u32[]{:S(2)}) collective-permute-start(bf16[2,128,256]{2,1,0:T(8,128)(2,1)S(1)} %pad_maximum_fusion.1), channel_id=1, source_target_pairs={{0,4},{2,6},{4,8},{6,10},{8,12},{10,14},{12,16},{14,18},{16,20},{1... | collective-permute-start | bytes 393224 | tf_op jit(solution)/shard_map/ppermute | solution.py:362
  86.3 7.6 %collective-permute-start.14 = (bf16[2,128,256]{2,1,0:T(8,128)(2,1)S(1)}, bf16[2,128,256]{2,1,0:T(8,128)(2,1)S(1)}, u32[]{:S(2)}, u32[]{:S(2)}) collective-permute-start(bf16[2,128,256]{2,1,0:T(8,128)(2,1)S(1)} %pad_maximum_fusion.1), channel_id=1, source_target_pairs={{0,2},{2,4},{4,6},{6,8},{8,10},{10,12},{12,14},{14,16},{16,18},{18... | collective-permute-start | bytes 393224 | tf_op jit(solution)/shard_map/ppermute | solution.py:362
  104.0 6.9 %copy-start.5 = (bf16[128,2048]{0,1:T(8,128)(2,1)S(1)}, bf16[128,2048]{0,1:T(8,128)(2,1)}, u32[]{:S(2)}) copy-start(bf16[128,2048]{0,1:T(8,128)(2,1)} %copy.28) | copy-start | bytes 1572868
  110.9 4.7 %copy-start.4 = (bf16[2048,1,128]{0,2,1:T(8,128)(2,1)S(1)}, bf16[2048,1,128]{0,2,1:T(8,128)(2,1)}, u32[]{:S(2)}) copy-start(bf16[2048,1,128]{0,2,1:T(8,128)(2,1)} %copy.40) | copy-start | bytes 1572868
  115.6 6.4 %copy-start.9 = (f32[8,128,2048]{1,2,0:T(8,128)S(1)}, f32[8,128,2048]{1,2,0:T(8,128)}, u32[]{:S(2)}) copy-start(f32[8,128,2048]{1,2,0:T(8,128)} %get-tuple-element.28) | copy-start | bytes 25165828
  122.0 23.0 %copy-start.2 = (bf16[128,2048]{1,0:T(8,128)(2,1)S(1)}, bf16[128,2048]{1,0:T(8,128)(2,1)}, u32[]{:S(2)}) copy-start(bf16[128,2048]{1,0:T(8,128)(2,1)} %param.15) | copy-start | bytes 1572868
  145.0 4.8 %copy-start.8 = (f32[2048]{0:T(1024)S(1)}, f32[2048]{0:T(1024)}, u32[]{:S(2)}) copy-start(f32[2048]{0:T(1024)} %param.17) | copy-start | bytes 24580
  (2 other events, 5.6 us)
Sparse Core Ops, SparseCore 0:
  10.8 134.1 all-gather.1

commit v2 on v1

--- a/solution.py
+++ b/solution.py
@@ -356,61 +356,224 @@
     )(normed, hidden_state, meta, gate_matrix, lift_matrix, down_matrix)
 
 
-def shifted(value, axis, steps):
-    count = lax.axis_size(axis)
-    initial, last = (max(0, -steps), min(count, count - steps))
-    return lax.ppermute(value, axis, [(source, source + steps) for source in range(initial, last)])
-
-
-def attend(queries, document_window, block_mask, block_extent):
-    total_row_count = queries.shape[0]
-    group_total = QUERY_HEADS // KEY_VALUE_HEADS
-    device = lax.axis_index("ctx")
-    per_block = MASK_BLOCK_SIZE // total_row_count
-    query_block = device // per_block
-    shard_device = device - (block_extent - 1) + jnp.arange(block_extent, dtype=jnp.int32)
-    shard_block = jnp.maximum(shard_device, 0) // per_block
-    mask_row = lax.dynamic_index_in_dim(block_mask, query_block, 0, keepdims=False)
-    block_ids = jnp.arange(block_mask.shape[1], dtype=jnp.int32)
-    lookup = jnp.sum(
-        jnp.where(shard_block[:, None] == block_ids[None, :], mask_row[None, :], 0), axis=1
-    )
-    shard_open = (shard_device >= 0) & (lookup == 1)
-    flat = jnp.arange(block_extent * total_row_count, dtype=jnp.int32)
-    shard_of = flat // total_row_count
-    place_of = flat % total_row_count
-    open_key = jnp.take(shard_open, shard_of)
-    query_place = jnp.arange(total_row_count, dtype=jnp.int32)
-    visible = open_key[None, :] & (
-        (shard_of[None, :] < block_extent - 1) | (place_of[None, :] <= query_place[:, None])
-    )
-    key_flattened = document_window[:, 0].reshape(
-        block_extent * total_row_count, KEY_VALUE_HEADS, HEAD_SIZE
-    )
-    value_flattened = document_window[:, 1].reshape(
-        block_extent * total_row_count, KEY_VALUE_HEADS, HEAD_SIZE
-    )
-    query_partition = queries.reshape(total_row_count, KEY_VALUE_HEADS, group_total, HEAD_SIZE)
-    outputs = []
-    for group_of_head in range(KEY_VALUE_HEADS):
-        scores = jnp.einsum(
-            "tgd,kd->gtk",
-            query_partition[:, group_of_head],
-            key_flattened[:, group_of_head],
-            preferred_element_type=jnp.float32,
-        ) / math.sqrt(HEAD_SIZE)
-        scores = jnp.where(visible[None], scores, -jnp.inf)
-        peak = jnp.max(scores, axis=-1, keepdims=True)
-        weights = jnp.exp(scores - peak)
-        probabilities = (weights / jnp.sum(weights, axis=-1, keepdims=True)).astype(jnp.bfloat16)
-        blended = jnp.einsum(
-            "gtk,kd->tgd",
-            probabilities,
-            value_flattened[:, group_of_head],
-            preferred_element_type=jnp.float32,
+NEG = -1e30
+
+
+def attn_kernel(
+    q_ref,
+    k_ref,
+    v_ref,
+    r_ref,
+    w_ref,
+    g_ref,
+    b_ref,
+    n_ref,
+    h_ref,
+    kbuf,
+    vbuf,
+    wfull,
+    bias,
+    s_ref,
+    p_ref,
+    l_ref,
+    att,
+    snd,
+    rcv,
+):
+    f32, bf16 = jnp.float32, jnp.bfloat16
+    tokens, width = q_ref.shape
+    me = lax.axis_index("ctx")
+    r = lax.axis_index("rep")
+    z = me // NQ
+    x, y = lax.rem(me, NQ) // NY, lax.rem(me, NY)
+    total = NQ * NZ
+    used = [0]
+
+    def at(dz, dx, dy):
+        return {"ctx": lax.rem(z + dz, NZ) * NQ + lax.rem(x + dx, NX) * NY + lax.rem(y + dy, NY)}
+
+    def later(j):
+        return {"ctx": lax.rem(me + j * NY, total)}
+
+    def send(src, dst, dev):
+        i = used[0]
+        used[0] += 1
+        c = pltpu.make_async_remote_copy(
+            src_ref=src, dst_ref=dst, send_sem=snd.at[i], recv_sem=rcv.at[i], device_id=dev, device_id_type=MESH_ID
         )
-        outputs.append(blended.astype(jnp.bfloat16))
-    return jnp.stack(outputs, axis=1).reshape(total_row_count, QUERY_HEADS * HEAD_SIZE)
+        c.start()
+        copies.append(c)
+        return c
+
+    copies = []
+    partner = {"rep": 1 - r}
+    barrier = pltpu.get_barrier_semaphore()
+    peers = [at(d, 0, 0) for d in range(1, NZ)] + [at(0, d, 0) for d in range(1, NX)] + [at(0, 0, d) for d in range(1, NY)]
+    peers += [partner] + [later(j) for j in range(1, DOCUMENT_BLOCKS)]
+    peers += [later(NQ * NZ // NY - j) for j in range(1, DOCUMENT_BLOCKS)]
+    for dev in peers:
+        pl.semaphore_signal(barrier, inc=1, device_id=dev, device_id_type=MESH_ID)
+    pl.semaphore_wait(barrier, len(peers))
+
+    def landed(cs):
+        for c in cs:
+            c.wait_recv()
+
+    order = (1, 3, 2)
+    half, quarter = width // 2, width // 4
+    pc, pa, pb = pl.ds(0, half), pl.ds(half, quarter), pl.ds(half + quarter, quarter)
+
+    k_next = {j: send(k_ref, kbuf.at[j, y], later(j)) for j in range(1, DOCUMENT_BLOCKS)}
+    v_row = [send(v_ref, vbuf.at[0, y], at(0, 0, d)) for d in order]
+    c_x = [send(w_ref.at[r, :, pc], wfull.at[z, x, y, r, :, pc], at(0, d, 0)) for d in order]
+    k_row = [send(k_ref, kbuf.at[0, y], at(0, 0, d)) for d in order]
+    z_order = (1, 7, 2, 6, 3, 5, 4)
+    a_z = [send(w_ref.at[r, :, pa], wfull.at[z, x, y, r, :, pa], at(d, 0, 0)) for d in z_order]
+    b_z = [send(w_ref.at[r, :, pb], wfull.at[z, x, y, r, :, pb], at(d, 0, 0)) for d in z_order]
+    kbuf[0, y] = k_ref[...]
+    vbuf[0, y] = v_ref[...]
+    wfull[z, x, y, r] = w_ref[r]
+
+    block = z * NX + x
+    for j in range(1, DOCUMENT_BLOCKS):
+        seen = (b_ref[block, jnp.maximum(block - j, 0)] == 1) & (block - j >= 0)
+        bias[:, j * MASK_BLOCK_SIZE : (j + 1) * MASK_BLOCK_SIZE] = jnp.full(
+            (tokens, MASK_BLOCK_SIZE), jnp.where(seen, 0.0, NEG), f32
+        )
+    for other in range(NY):
+        rows = lax.broadcasted_iota(jnp.int32, (tokens, tokens), 0) + (y - other) * tokens
+        cols = lax.broadcasted_iota(jnp.int32, (tokens, tokens), 1)
+        bias[:, other * tokens : (other + 1) * tokens] = jnp.where(cols <= rows, 0.0, NEG)
+
+    for j in range(1, DOCUMENT_BLOCKS):
+        k_next[j].wait_recv()
+        k_row += [send(kbuf.at[j, y], kbuf.at[j, y], at(0, 0, d)) for d in order]
+    landed(v_row)
+    v_next = [send(vbuf.at[0], vbuf.at[j], later(j)) for j in range(1, DOCUMENT_BLOCKS)]
+    landed(c_x)
+    c_y = [send(wfull.at[z, :, y, r, :, pc], wfull.at[z, :, y, r, :, pc], at(0, 0, d)) for d in order]
+    landed(a_z)
+    a_x = [send(wfull.at[:, x, y, r, :, pa], wfull.at[:, x, y, r, :, pa], at(0, d, 0)) for d in order]
+    landed(b_z)
+    b_y = [send(wfull.at[:, x, y, r, :, pb], wfull.at[:, x, y, r, :, pb], at(0, 0, d)) for d in order]
+    landed(c_y)
+
+    def ring(k, d):
+        zz = lax.rem(z + (NZ - k if d == 0 else k), NZ)
+        xs = pl.ds(0, NX) if k < 3 else pl.ds(2 * d, 2)
+        piece = wfull.at[zz, xs, :, r, :, pc]
+        return send(piece, piece, at(1 if d == 0 else NZ - 1, 0, 0))
+
+    def share(piece):
+        return send(piece, piece, partner)
+
+    c_z = [ring(0, 0), ring(0, 1)]
+    shared = [share(wfull.at[z, :, :, r, :, pc])]
+    landed(a_x)
+    a_y = [send(wfull.at[:, :, y, r, :, pa], wfull.at[:, :, y, r, :, pa], at(0, 0, d)) for d in order]
+    landed(b_y)
+    b_x = [send(wfull.at[:, x, :, r, :, pb], wfull.at[:, x, :, r, :, pb], at(0, d, 0)) for d in order]
+
+    def forward(k):
+        for d in range(2):
+            c_z[d].wait_recv()
+            if k < 4:
+                c_z[d] = ring(k, d)
+            zz = lax.rem(z + (NZ - k if d == 0 else k), NZ)
+            xs = pl.ds(0, NX) if k < 4 else pl.ds(2 * d, 2)
+            shared.append(share(wfull.at[zz, xs, :, r, :, pc]))
+
+    landed(k_row)
+    landed(v_next)
+
+    factor = math.log2(math.e) / math.sqrt(HEAD_SIZE)
+    keys_all = DOCUMENT_BLOCKS * MASK_BLOCK_SIZE
+
+    def heads(hp, carry):
+        first = pl.multiple_of(hp * 2 * HEAD_SIZE, 2 * HEAD_SIZE)
+        group = pl.ds(pl.multiple_of((hp // 4) * HEAD_SIZE, HEAD_SIZE), HEAD_SIZE)
+        one = pl.ds(first, HEAD_SIZE)
+        two = pl.ds(first + HEAD_SIZE, HEAD_SIZE)
+        both = jnp.concatenate([q_ref[:, one], q_ref[:, two]], axis=0)
+        kk = kbuf[:, :, :, group].reshape(keys_all, HEAD_SIZE)
+        s_ref[...] = lax.dot_general(both, kk, (((1,), (1,)), ((), ())), preferred_element_type=f32)
+
+        def soft(i, inner):
+            rows = pl.ds(pl.multiple_of(i * 16, 16), 16)
+            v = s_ref[rows, :] + bias[pl.ds(pl.multiple_of(lax.rem(i, 8) * 16, 16), 16), :]
+            m = jnp.max(v, axis=1, keepdims=True)
+            e = jnp.exp2((v - m) * factor)
+            l_ref[rows, :] = jnp.broadcast_to(jnp.sum(e, axis=1, keepdims=True), (16, HEAD_SIZE))
+            p_ref[rows, :] = e.astype(bf16)
+            return inner
+
+        lax.fori_loop(0, 16, soft, 0)
+        vv = vbuf[:, :, :, group].reshape(keys_all, HEAD_SIZE)
+        o = jnp.dot(p_ref[...], vv, preferred_element_type=f32) / l_ref[...]
+        att[:, one] = o[:tokens].astype(bf16)
+        att[:, two] = o[tokens:].astype(bf16)
+        return carry
+
+    for k in range(1, 5):
+        lax.fori_loop(2 * k - 2, 2 * k, heads, 0)
+        forward(k)
+    landed(a_y)
+    shared.append(share(wfull.at[:, :, :, r, :, pa]))
+    landed(b_x)
+    shared.append(share(wfull.at[:, :, :, r, :, pb]))
+    landed(shared)
+
+    tile = 256
+
+    def project(c, squares):
+        cols = pl.ds(pl.multiple_of(c * tile, tile), tile)
+        w = wfull[:, :, :, :, :, cols].reshape(width, tile)
+        out = jnp.dot(att[...], w, preferred_element_type=f32) + r_ref[:, cols].astype(f32)
+        out = out.astype(bf16)
+        h_ref[:, cols] = out
+        wide = out.astype(f32)
+        return squares + jnp.sum(wide * wide, axis=1, keepdims=True)
+
+    squares = lax.fori_loop(0, width // tile, project, jnp.zeros((tokens, 1), f32))
+    scale = lax.rsqrt(squares / width + 1e-06)
+
+    def norm(c, carry):
+        cols = pl.ds(pl.multiple_of(c * tile, tile), tile)
+        n_ref[:, cols] = (h_ref[:, cols].astype(f32) * scale * g_ref[:, cols]).astype(bf16)
+        return carry
+
+    lax.fori_loop(0, width // tile, norm, 0)
+    for c in copies:
+        c.wait_send()
+
+
+def attention(queries, keys, values, residual, out_matrix, norm_gain, block_mask):
+    rows, width = queries.shape
+    bf16, f32 = jnp.bfloat16, jnp.float32
+    vmem = pl.BlockSpec(memory_space=pltpu.VMEM)
+    group = keys.shape[1]
+    reach = DOCUMENT_BLOCKS * MASK_BLOCK_SIZE
+    shape = jax.ShapeDtypeStruct((rows, width), bf16)
+    return pl.pallas_call(
+        attn_kernel,
+        out_shape=(shape, shape),
+        in_specs=[vmem] * 6 + [pl.BlockSpec(memory_space=pltpu.SMEM)],
+        out_specs=(vmem, vmem),
+        scratch_shapes=[
+            pltpu.VMEM((DOCUMENT_BLOCKS, NY, rows, group), bf16),
+            pltpu.VMEM((DOCUMENT_BLOCKS, NY, rows, group), bf16),
+            pltpu.VMEM((NZ, NX, NY, 2, 8, width), bf16),
+            pltpu.VMEM((rows, reach), f32),
+            pltpu.VMEM((2 * rows, reach), f32),
+            pltpu.VMEM((2 * rows, reach), bf16),
+            pltpu.VMEM((2 * rows, HEAD_SIZE), f32),
+            pltpu.VMEM((rows, width), bf16),
+            pltpu.SemaphoreType.DMA((80,)),
+            pltpu.SemaphoreType.DMA((80,)),
+        ],
+        compiler_params=pltpu.CompilerParams(collective_id=1, has_side_effects=True, vmem_limit_bytes=60 * 1024 * 1024),
+        name="attn",
+    )(queries, keys, values, residual, out_matrix.reshape(2, 8, width), norm_gain.reshape(1, width), block_mask)
 
 
 def shards(
@@ -427,24 +590,9 @@
     down_matrix,
     block_mask,
 ):
-    total_row_count = queries.shape[0]
-    devices = lax.axis_size("ctx")
-    block_extent = DOCUMENT_BLOCKS * MASK_BLOCK_SIZE // total_row_count
-    model_width = out_matrix.shape[1]
-    paired = jnp.stack([encoded_key_heads, value_head_vectors])
-    earlier = [shifted(paired, "ctx", distance) for distance in range(block_extent - 1, 0, -1)]
-    document_window = jnp.stack(earlier + [paired])
-    attended = attend(queries, document_window, block_mask, block_extent)
-    projected = jnp.dot(
-        attended,
-        lax.all_gather(out_matrix, "ctx", axis=0, tiled=True),
-        preferred_element_type=jnp.float32,
+    normed, hidden_state = attention(
+        queries, encoded_key_heads, value_head_vectors, residual, out_matrix, norm_gain, block_mask
     )
-    hidden_state = (residual.astype(jnp.float32) + projected).astype(jnp.bfloat16)
-    widened = hidden_state.astype(jnp.float32)
-    normed = (
-        widened * lax.rsqrt(jnp.mean(widened * widened, axis=-1, keepdims=True) + 1e-06) * norm_gain
-    ).astype(jnp.bfloat16)
     meta = jnp.concatenate([expert_ids.astype(jnp.float32).T, expert_gates.T])
     return moe(normed, hidden_state, meta, gate_matrix, lift_matrix, down_matrix)
 

time: 294 us -> 230 us (0.78)
  Pallas kernels: 134 us -> 225 us
  starting transfers between devices: 65.2 us -> 0 us
  waiting for transfers between devices: 25.7 us -> 0 us
  matrix products: 21.6 us -> 0 us
  local copies, waits for them, and re-layouts: 16.8 us -> 1.88 us
  other arithmetic: 16.3 us -> 1.97 us
  between operations: 13.9 us -> 0.02 us
    pallas_call x0 -> x1, Pallas kernels: none -> 73.5 us  [attention(): pl.pallas_call(attn_kernel, out_shape=(shape, shape), in_specs=[vmem] * 6...]
    ppermute x15 -> x0, starting transfers between devices: 65.2 us -> none  [shifted(): lax.ppermute(value, axis, [(source, source + steps) for source in range(i...]
    all_gather x1 -> x0, waiting for transfers between devices: 22.2 us -> none  [shards(): lax.all_gather(out_matrix, 'ctx', axis=0, tiled=True)]
    pallas_call x1, Pallas kernels: 134 us -> 152 us  [moe(): pl.pallas_call(moe_kernel, out_shape=jax.ShapeDtypeStruct((rows, width),...]
    sub x2 -> x0, matrix products: 11.5 us -> none  [attend(): weights = jnp.exp(scores - peak)]
    dot_general x3 -> x0, matrix products: 10.1 us -> none  [the longest x2 5.28 us: attend(): jnp.einsum('gtk,kd->tgd', probabilities, value_flattened[:, group_of_head...]
    unnamed x39 -> x1, local copies, waits for them, and re-layouts: 11.3 us -> 1.88 us
    lt x1 -> x0, other arithmetic: 5.57 us -> none  [attend(): shard_of[None, :] < block_extent - 1]
  transfers between devices with their start and end apart: 16 -> 0, of which waited for: 2 -> 0; matrix products, arithmetic and copies ran while one was open for 15% -> 0% of each run, Pallas kernels for 0% -> 0%
where the time goes in v2:
time: 230 us; the launch traced here: 229 us
  Pallas kernels  225 us (98%)
    pallas_call x1, Pallas kernels, moe(): pl.pallas_call(moe_kernel, out_shape=jax.ShapeDtypeStruct((rows, width),...  152 us
    pallas_call x1, Pallas kernels, attention(): pl.pallas_call(attn_kernel, out_shape=(shape, shape), in_specs=[vmem] * 6...  73.5 us

profile of v2, /device:TPU:8, one launch (start us, length us, event | category | flops | bytes accessed | tf_op | source)
XLA Modules:
  0.0 229.4 jit_solution(13200925467673702515)
XLA Ops:
  0.0 0.7 convert_bitcast_fusion
  0.7 1.3 pad_maximum_fusion.m_ref
  2.0 73.5 %attn.1 = (bf16[128,2048]{1,0:T(8,128)(2,1)}, bf16[128,2048]{1,0:T(8,128)(2,1)}) custom-call(bf16[128,2048]{1,0:T(8,128)(2,1)} %q_ref.1, bf16[128,256]{1,0:T(8,128)(2,1)} %k_ref.1, bf16[128,256]{1,0:T(8,128)(2,1)} %v_ref.1, bf16[128,2048]{1,0:T(8,128)(2,1)} %r_ref.1, bf16[2,8,2048]{2,1,0:T(8,128)(2,1)} %bitcast.5, f32[1,2048]{1,0:T(1,128)} %bitcast.6, ...), custom_call_target="tpu_custom_call" | custom-call | tf_op jit(solution)/shard_map/attn/pallas_call | solution.py:557
  75.5 152.0 %moe.1 = bf16[128,2048]{1,0:T(8,128)(2,1)} custom-call(bf16[128,2048]{1,0:T(8,128)(2,1)} %get-tuple-element.7.x_ref, bf16[128,2048]{1,0:T(8,128)(2,1)} %get-tuple-element.8.h_ref, f32[16,128]{1,0:T(8,128)} %pad_maximum_fusion.m_ref, bf16[1,2048,768]{2,1,0:T(8,128)(2,1)} %wg_hbm.1, bf16[1,2048,768]{2,1,0:T(8,128)(2,1)} %wl_hbm.1, bf16[1,768,2048]{2,1,0:T(8,128)(2,1)} %wd_hbm.1), custom_call_target="tpu_custom_call" | custom-call | tf_op jit(solution)/shard_map/moe/pallas_call | solution.py:321
  227.5 1.9 copy.14

commit v3 on v1

v3 whole, which is shorter than its diff:
```python
import math

import jax
import jax.numpy as jnp
from jax import lax
from jax.experimental import pallas as pl
from jax.experimental.pallas import tpu as pltpu
from jax.sharding import PartitionSpec as P

QUERY_HEADS = 16
KEY_VALUE_HEADS = 2
HEAD_SIZE = 128
TOP = 8
MASK_BLOCK_SIZE = 512
DOCUMENT_BLOCKS = 4


MESH_ID = pl.DeviceIdType.MESH
PLANE = ((1, 0), (3, 0), (0, 1), (0, 3), (1, 1), (3, 3), (1, 3), (3, 1), (2, 0), (0, 2), (2, 1), (2, 3), (1, 2), (3, 2), (2, 2))
CAP = 9
NX, NY, NZ = 4, 4, 8
NQ = NX * NY
NEG = -1e30
COPIES = 112


def layer_kernel(
    q_ref,
    k_ref,
    v_ref,
    r_ref,
    w_ref,
    g_ref,
    b_ref,
    i_ref,
    t_ref,
    wg_hbm,
    wl_hbm,
    wd_hbm,
    o_ref,
    kbuf,
    vbuf,
    wfull,
    bias,
    s_ref,
    p_ref,
    l_ref,
    att,
    snd,
    rcv,
    h_ref,
    ids,
    gates,
    wg,
    wl,
    wd,
    xg,
    keys,
    gts,
    outbox,
    inbox,
    ret,
    xs,
    act,
    part,
    rsend,
    rrecv,
    w_sem,
    zs,
    zr,
    ds_,
    dr,
    bs,
    br,
    ss,
    sr,
):
    f32, bf16 = jnp.float32, jnp.bfloat16
    tokens, width = q_ref.shape
    me = lax.axis_index("ctx")
    r = lax.axis_index("rep")
    z = me // NQ
    q = lax.rem(me, NQ)
    x, y = q // NY, lax.rem(q, NY)
    total = NQ * NZ
    used = [0]

    def at(dz, dx, dy):
        return {"ctx": lax.rem(z + dz, NZ) * NQ + lax.rem(x + dx, NX) * NY + lax.rem(y + dy, NY)}

    def later(j):
        return {"ctx": lax.rem(me + j * NY, total)}

    def send(src, dst, dev):
        i = used[0]
        used[0] += 1
        c = pltpu.make_async_remote_copy(
            src_ref=src, dst_ref=dst, send_sem=snd.at[i], recv_sem=rcv.at[i], device_id=dev, device_id_type=MESH_ID
        )
        c.start()
        copies.append(c)
        return c

    weights = [
        pltpu.make_async_copy(a, b, w_sem.at[i])
        for i, (a, b) in enumerate(((wg_hbm.at[0], wg), (wl_hbm.at[0], wl), (wd_hbm.at[0], wd)))
    ]
    for c in weights:
        c.start()

    copies = []
    partner = {"rep": 1 - r}
    barrier = pltpu.get_barrier_semaphore()
    peers = [at(d, 0, 0) for d in range(1, NZ)] + [at(0, d, 0) for d in range(1, NX)] + [at(0, 0, d) for d in range(1, NY)]
    peers += [partner] + [later(j) for j in range(1, DOCUMENT_BLOCKS)]
    peers += [later(NQ * NZ // NY - j) for j in range(1, DOCUMENT_BLOCKS)]
    peers += [at(0, a, b) for a, b in PLANE]
    for dev in peers:
        pl.semaphore_signal(barrier, inc=1, device_id=dev, device_id_type=MESH_ID)
    pl.semaphore_wait(barrier, len(peers))

    def landed(cs):
        for c in cs:
            c.wait_recv()

    order = (1, 3, 2)
    z_order = (1, 7, 2, 6, 3, 5, 4)
    part_c, part_a = 3 * width // 8, 5 * width // 16
    pc, pa, pb = pl.ds(0, part_c), pl.ds(part_c, part_a), pl.ds(part_c + part_a, part_a)

    c_x = [send(w_ref.at[r, :, pc], wfull.at[z, x, y, r, :, pc], at(0, d, 0)) for d in order]
    k_next = {j: send(k_ref, kbuf.at[j, y], later(j)) for j in range(1, DOCUMENT_BLOCKS)}
    v_row = [send(v_ref, vbuf.at[0, y], at(0, 0, d)) for d in order]
    a_z = [send(w_ref.at[r, :, pa], wfull.at[z, x, y, r, :, pa], at(d, 0, 0)) for d in z_order]
    b_z = [send(w_ref.at[r, :, pb], wfull.at[z, x, y, r, :, pb], at(d, 0, 0)) for d in z_order]
    slot_of = {1: 1, 7: 2, 2: 3, 6: 4, 3: 5, 5: 6, 4: 7}
    tables = []
    for d in z_order:
        tables.append(send(i_ref, ids.at[slot_of[d]], at(d, 0, 0)))
        tables.append(send(t_ref, gates.at[slot_of[d]], at(d, 0, 0)))
    ids[0] = i_ref[...]
    gates[0] = t_ref[...]
    kbuf[0, y] = k_ref[...]
    vbuf[0, y] = v_ref[...]
    wfull[z, x, y, r] = w_ref[r]
    shared = []

    def share(piece):
        shared.append(send(piece, piece, partner))

    landed(c_x)
    c_y = [send(wfull.at[z, :, y, r, :, pc], wfull.at[z, :, y, r, :, pc], at(0, 0, d)) for d in order]
    k_row = [send(k_ref, kbuf.at[0, y], at(0, 0, d)) for d in order]
    for j in range(1, DOCUMENT_BLOCKS):
        k_next[j].wait_recv()
        k_row += [send(kbuf.at[j, y], kbuf.at[j, y], at(0, 0, d)) for d in order]
    landed(v_row)
    v_next = [send(vbuf.at[0], vbuf.at[j], later(j)) for j in range(1, DOCUMENT_BLOCKS)]

    def plane(k, d):
        return lax.rem(z + (NZ - k if d == 0 else k), NZ)

    def ring_parts(k):
        return [(d, e) for e in range(2) for d in range(2) if k < 3 or d == e]

    def ring_piece(k, d, e):
        return wfull.at[plane(k, d), pl.ds(2 * e, 2), :, r, :, pc]

    def ring(k, d, e):
        piece = ring_piece(k, d, e)
        return send(piece, piece, at(1 if d == 0 else NZ - 1, 0, 0))

    landed(c_y)
    c_z = {(d, e): ring(0, d, e) for d, e in ring_parts(0)}
    share(wfull.at[z, :, :, r, :, pc])

    def forward(k):
        for d, e in ring_parts(k - 1):
            c_z[d, e].wait_recv()
            if k < 4 and (d, e) in ring_parts(k):
                c_z[d, e] = ring(k, d, e)
            share(ring_piece(k, d, e))

    landed(a_z)
    a_x = [send(wfull.at[:, x, y, r, :, pa], wfull.at[:, x, y, r, :, pa], at(0, d, 0)) for d in order]
    landed(b_z)
    b_y = [send(wfull.at[:, x, y, r, :, pb], wfull.at[:, x, y, r, :, pb], at(0, 0, d)) for d in order]

    def last_a(i, zs):
        return wfull.at[zs, :, i, r, :, pa]

    def last_b(i, zs):
        return wfull.at[zs, i, :, r, :, pb]

    every = pl.ds(0, NZ)

    def step(of, i, d, zs):
        piece = of(i, zs)
        shift = 1 if d == 0 else NY - 1
        return send(piece, piece, at(0, 0, shift) if of is last_a else at(0, shift, 0))

    def begin(of, i):
        share(of(i, every))
        return [step(of, i, d, every) for d in range(2)]

    def pass_on(of, i, first):
        second = []
        for d in range(2):
            first[d].wait_recv()
            came = lax.rem(i + (NY - 1 if d == 0 else 1), NY)
            second.append(step(of, came, d, pl.ds(4 * d, 4)))
            share(of(came, every))
        return second

    def finish(of, i, second):
        for d in range(2):
            second[d].wait_recv()
            share(of(lax.rem(i + 2, NY), pl.ds(4 * d, 4)))

    block = z * NX + x
    for j in range(1, DOCUMENT_BLOCKS):
        seen = (b_ref[block, jnp.maximum(block - j, 0)] == 1) & (block - j >= 0)
        bias[:, j * MASK_BLOCK_SIZE : (j + 1) * MASK_BLOCK_SIZE] = jnp.full(
            (tokens, MASK_BLOCK_SIZE), jnp.where(seen, 0.0, NEG), f32
        )
    for other in range(NY):
        rows = lax.broadcasted_iota(jnp.int32, (tokens, tokens), 0) + (y - other) * tokens
        cols = lax.broadcasted_iota(jnp.int32, (tokens, tokens), 1)
        bias[:, other * tokens : (other + 1) * tokens] = jnp.where(cols <= rows, 0.0, NEG)


    landed(a_x)
    a_last = begin(last_a, y)
    landed(b_y)
    b_last = begin(last_b, x)
    forward(1)
    landed(tables)
    tri = (
        lax.broadcasted_iota(jnp.int32, (tokens, tokens), 0) < lax.broadcasted_iota(jnp.int32, (tokens, tokens), 1)
    ).astype(bf16)
    expert = (lax.broadcasted_iota(jnp.int32, (NQ, tokens), 0) + z * NQ)

    def block_keys(b):
        named, weight = ids[b], gates[b]
        chosen = jnp.zeros((NQ, tokens), f32)
        gate = jnp.zeros((NQ, tokens), f32)
        for k in range(TOP):
            hit = expert == named[k : k + 1, :]
            chosen = jnp.where(hit, 1.0, chosen)
            gate = jnp.where(hit, weight[k : k + 1, :], gate)
        rank = jnp.dot(chosen.astype(bf16), tri, preferred_element_type=f32)
        keys[b] = jnp.where(chosen > 0.5, rank, -100.0)
        gts[b] = gate

    def all_keys(b, carry):
        block_keys(b)
        return carry

    lax.fori_loop(0, NZ, all_keys, 0)
    landed(k_row)
    landed(v_next)
    forward(2)

    factor = math.log2(math.e) / math.sqrt(HEAD_SIZE)
    keys_all = DOCUMENT_BLOCKS * MASK_BLOCK_SIZE

    def heads(hp, carry):
        first = pl.multiple_of(hp * 2 * HEAD_SIZE, 2 * HEAD_SIZE)
        group = pl.ds(pl.multiple_of((hp // 4) * HEAD_SIZE, HEAD_SIZE), HEAD_SIZE)
        one = pl.ds(first, HEAD_SIZE)
        two = pl.ds(first + HEAD_SIZE, HEAD_SIZE)
        both = jnp.concatenate([q_ref[:, one], q_ref[:, two]], axis=0)
        kk = kbuf[:, :, :, group].reshape(keys_all, HEAD_SIZE)
        s_ref[...] = lax.dot_general(both, kk, (((1,), (1,)), ((), ())), preferred_element_type=f32)

        def soft(i, inner):
            rows = pl.ds(pl.multiple_of(i * 16, 16), 16)
            v = s_ref[rows, :] + bias[pl.ds(pl.multiple_of(lax.rem(i, 8) * 16, 16), 16), :]
            m = jnp.max(v, axis=1, keepdims=True)
            e = jnp.exp2((v - m) * factor)
            l_ref[rows, :] = jnp.broadcast_to(jnp.sum(e, axis=1, keepdims=True), (16, HEAD_SIZE))
            p_ref[rows, :] = e.astype(bf16)
            return inner

        lax.fori_loop(0, 16, soft, 0, unroll=8)
        vv = vbuf[:, :, :, group].reshape(keys_all, HEAD_SIZE)
        o = jnp.dot(p_ref[...], vv, preferred_element_type=f32) / l_ref[...]
        att[:, one] = o[:tokens].astype(bf16)
        att[:, two] = o[tokens:].astype(bf16)
        return carry

    lax.fori_loop(0, 2, heads, 0)
    a_end = pass_on(last_a, y, a_last)
    b_end = pass_on(last_b, x, b_last)
    forward(3)
    lax.fori_loop(2, 5, heads, 0)
    forward(4)
    finish(last_a, y, a_end)
    finish(last_b, x, b_end)
    lax.fori_loop(5, 8, heads, 0)
    landed(shared)

    tile = 256

    def project(c, squares):
        cols = pl.ds(pl.multiple_of(c * tile, tile), tile)
        w = wfull[:, :, :, :, :, cols].reshape(width, tile)
        out = jnp.dot(att[...], w, preferred_element_type=f32) + r_ref[:, cols].astype(f32)
        out = out.astype(bf16)
        h_ref[:, cols] = out
        wide = out.astype(f32)
        return squares + jnp.sum(wide * wide, axis=1, keepdims=True)

    squares = lax.fori_loop(0, width // tile, project, jnp.zeros((tokens, 1), f32))
    scale = lax.rsqrt(squares / width + 1e-06)

    def norm(c, carry):
        cols = pl.ds(pl.multiple_of(c * tile, tile), tile)
        xg[0, :, cols] = (h_ref[:, cols].astype(f32) * scale * g_ref[:, cols]).astype(bf16)
        return carry

    lax.fori_loop(0, width // tile, norm, 0)

    half = tokens // 2

    def zpeer(d):
        return lax.rem(z + d, NZ) * NQ + q

    def qpeer(i):
        return lax.rem(x + PLANE[i][0], NX) * NY + lax.rem(y + PLANE[i][1], NY)

    def remote(src, dst, s_sem, r_sem, dev):
        return pltpu.make_async_remote_copy(
            src_ref=src, dst_ref=dst, send_sem=s_sem, recv_sem=r_sem, device_id={"ctx": dev}, device_id_type=MESH_ID
        )

    def zcopy(d, k, h):
        src = xg.at[0] if k == 0 else xg.at[2 * k - 1 + d]
        rows = pl.ds(h * half, half)
        dst = xg.at[2 * k + 1 + d] if k < 3 else xg.at[7]
        return remote(src.at[rows], dst.at[rows], zs.at[d, k, h], zr.at[d, k, h], zpeer(1 if d == 0 else NZ - 1))

    def zparts(k):
        return [(d, h) for h in range(2) for d in range(2) if k < 3 or d == h]

    for d, h in zparts(0):
        zcopy(d, 0, h).start()
    row = lax.broadcasted_iota(jnp.int32, (NQ, 8, tokens), 1)

    def hits(b, first):
        return keys[b][:, None, :] == (row + first).astype(f32)

    def pick(b, first):
        return jnp.where(hits(b, first), 1.0, 0.0).reshape(NQ * 8, tokens).astype(bf16)

    def build(t, blocks):
        mats = [pick(b, first) for b, first in blocks]
        chunk = width // 4

        def piece(c, carry):
            cols = pl.ds(pl.multiple_of(c * chunk, chunk), chunk)
            total = None
            for (b, _), mat in zip(blocks, mats):
                one = jnp.dot(mat, xg[b, :, cols], preferred_element_type=f32)
                total = one if total is None else total + one
            outbox[t, :, :, cols] = total.astype(bf16).reshape(NQ, 8, chunk)
            return carry

        lax.fori_loop(0, 4, piece, 0)
        for i in range(NQ - 1):
            p = qpeer(i)
            remote(outbox.at[t, p], inbox.at[t, q], ds_.at[t], dr.at[t], z * NQ + p).start()
        inbox[t, q] = outbox[t, q]

    def dispatch(t):
        if isinstance(t, int) and t == 0:
            build(0, [(0, 0)])
        elif isinstance(t, int) and t == 8:
            build(8, [(7, 1)])
        else:
            build(t, [(t - 1, 9 - t), (t, -t)])

    def wait_all(buf, sem):
        pltpu.make_async_copy(buf, buf, sem).wait()

    def mlp(first, count):
        rows = count * NQ * 8

        def take(t, carry):
            wait_all(inbox.at[first + t, pl.ds(0, NQ - 1)], dr.at[first + t])
            xs[pl.ds(pl.multiple_of(t * NQ * 8, NQ * 8), NQ * 8), :] = inbox[first + t].reshape(NQ * 8, width)
            return carry

        lax.fori_loop(0, count, take, 0)
        hidden = wg.shape[1]
        tile = 256

        def up(c, carry):
            cols = pl.ds(pl.multiple_of(c * tile, tile), tile)
            g = jnp.dot(xs[pl.ds(0, rows), :], wg[:, cols], preferred_element_type=f32)
            u = jnp.dot(xs[pl.ds(0, rows), :], wl[:, cols], preferred_element_type=f32)
            act[pl.ds(0, rows), cols] = (g / (1.0 + jnp.exp(-g)) * u).astype(bf16)
            return carry

        lax.fori_loop(0, hidden // tile, up, 0)

        def down(c, carry):
            cols = pl.ds(pl.multiple_of(c * tile, tile), tile)
            y = jnp.dot(act[pl.ds(0, rows), :], wd[:, cols], preferred_element_type=f32)
            inbox[pl.ds(first, count), :, :, cols] = y.astype(bf16).reshape(count, NQ, 8, tile)
            return carry

        lax.fori_loop(0, width // tile, down, 0)

    def give_back(t):
        for i in range(NQ - 1):
            p = qpeer(i)
            remote(inbox.at[t, p], ret.at[t, q], bs.at[t], br.at[t], z * NQ + p).start()
        ret[t, q] = inbox[t, q]

    dispatch(0)
    groups = ((0, 3), (3, 2), (5, 2), (7, 2))
    for k in range(4):
        for d, h in zparts(k):
            zcopy(d, k, h).wait_recv()
            if k < 3 and (d, h) in zparts(k + 1):
                zcopy(d, k + 1, h).start()
        if k < 3:

            def two(t, carry):
                dispatch(t)
                return carry

            lax.fori_loop(2 * k + 1, 2 * k + 3, two, 0)
        else:
            dispatch(7)
            dispatch(8)
        if k == 0:
            for c in weights:
                c.wait()
        else:
            mlp(*groups[k - 1])
    mlp(*groups[3])

    def back(t, carry):
        give_back(8 - t)
        return carry

    lax.fori_loop(0, 9, back, 0)

    def wait_ret(t):
        wait_all(ret.at[t, pl.ds(0, NQ - 1)], br.at[t])

    def partial(b, slot):
        lo = jnp.where(hits(b, -b), gts[b][:, None, :], 0.0).reshape(NQ * 8, tokens)
        hi = jnp.where(hits(b, 8 - b), gts[b][:, None, :], 0.0).reshape(NQ * 8, tokens)
        mat = jnp.concatenate([lo, hi], axis=0).T.astype(bf16)
        chunk = width // 4

        def piece(c, carry):
            cols = pl.ds(pl.multiple_of(c * chunk, chunk), chunk)
            rows = ret[b : b + 2, :, :, cols].reshape(2 * NQ * 8, chunk)
            part[slot, :, cols] = jnp.dot(mat, rows, preferred_element_type=f32)
            return carry

        lax.fori_loop(0, 4, piece, 0)

    def scopy(d, k, h):
        rows = pl.ds(h * half, half)
        return remote(
            rsend.at[d, k, rows], rrecv.at[d, k, rows], ss.at[d, k, h], sr.at[d, k, h], zpeer(1 if d == 0 else NZ - 1)
        )

    def sparts(k):
        return [(d, h) for h in range(2) for d in range(2) if k > 0 or d == h]

    wait_ret(8)
    wait_ret(7)
    partial(7, 0)
    for d, h in sparts(0):
        rows = pl.ds(h * half, half)
        rsend[d, 0, rows] = part[0, rows].astype(bf16)
        scopy(d, 0, h).start()
    for k in range(1, 4):
        wait_ret(8 - 2 * k)
        wait_ret(7 - 2 * k)
        partial(8 - 2 * k, 0)
        partial(7 - 2 * k, 1)
        for d, h in sparts(k):
            rows = pl.ds(h * half, half)
            total = part[d, rows]
            if (d, h) in sparts(k - 1):
                scopy(d, k - 1, h).wait_recv()
                total = total + rrecv[d, k - 1, rows].astype(f32)
            rsend[d, k, rows] = total.astype(bf16)
            scopy(d, k, h).start()
    wait_ret(0)
    partial(0, 0)
    for h in range(2):
        rows = pl.ds(h * half, half)
        total = part[0, rows] + h_ref[rows, :].astype(f32)
        for d in range(2):
            scopy(d, 3, h).wait_recv()
            total = total + rrecv[d, 3, rows].astype(f32)
        o_ref[rows, :] = total.astype(bf16)

    for c in copies:
        c.wait_send()
    for k in range(4):
        for d, h in zparts(k):
            zcopy(d, k, h).wait_send()
        for d, h in sparts(k):
            scopy(d, k, h).wait_send()

    def sent(t, carry):
        wait_all(outbox.at[t, pl.ds(0, NQ - 1)], ds_.at[t])
        wait_all(inbox.at[t, pl.ds(0, NQ - 1)], bs.at[t])
        return carry

    lax.fori_loop(0, 9, sent, 0)


def layer(queries, keys, values, residual, out_matrix, norm_gain, block_mask, ids, gates, gate_matrix, lift_matrix, down_matrix):
    rows, width = queries.shape
    bf16, f32 = jnp.bfloat16, jnp.float32
    vmem = pl.BlockSpec(memory_space=pltpu.VMEM)
    hbm = pl.BlockSpec(memory_space=pl.ANY)
    dma = pltpu.SemaphoreType.DMA
    group, ff = keys.shape[1], gate_matrix.shape[2]
    reach = DOCUMENT_BLOCKS * MASK_BLOCK_SIZE
    return pl.pallas_call(
        layer_kernel,
        out_shape=jax.ShapeDtypeStruct((rows, width), bf16),
        in_specs=[vmem] * 6 + [pl.BlockSpec(memory_space=pltpu.SMEM), vmem, vmem, hbm, hbm, hbm],
        out_specs=vmem,
        scratch_shapes=[
            pltpu.VMEM((DOCUMENT_BLOCKS, NY, rows, group), bf16),
            pltpu.VMEM((DOCUMENT_BLOCKS, NY, rows, group), bf16),
            pltpu.VMEM((NZ, NX, NY, 2, 8, width), bf16),
            pltpu.VMEM((rows, reach), f32),
            pltpu.VMEM((2 * rows, reach), f32),
            pltpu.VMEM((2 * rows, reach), bf16),
            pltpu.VMEM((2 * rows, HEAD_SIZE), f32),
            pltpu.VMEM((rows, width), bf16),
            dma((COPIES,)),
            dma((COPIES,)),
            pltpu.VMEM((rows, width), bf16),
            pltpu.VMEM((NZ, TOP, rows), jnp.int32),
            pltpu.VMEM((NZ, TOP, rows), f32),
            pltpu.VMEM((width, ff), bf16),
            pltpu.VMEM((width, ff), bf16),
            pltpu.VMEM((ff, width), bf16),
            pltpu.VMEM((NZ, rows, width), bf16),
            pltpu.VMEM((NZ, NQ, rows), f32),
            pltpu.VMEM((NZ, NQ, rows), f32),
            pltpu.VMEM((CAP, NQ, 8, width), bf16),
            pltpu.VMEM((CAP, NQ, 8, width), bf16),
            pltpu.VMEM((CAP, NQ, 8, width), bf16),
            pltpu.VMEM((3 * NQ * 8, width), bf16),
            pltpu.VMEM((3 * NQ * 8, ff), bf16),
            pltpu.VMEM((2, rows, width), f32),
            pltpu.VMEM((2, 4, rows, width), bf16),
            pltpu.VMEM((2, 4, rows, width), bf16),
            dma((3,)),
            dma((2, 4, 2)),
            dma((2, 4, 2)),
            dma((CAP,)),
            dma((CAP,)),
            dma((CAP,)),
            dma((CAP,)),
            dma((2, 4, 2)),
            dma((2, 4, 2)),
        ],
        compiler_params=pltpu.CompilerParams(collective_id=0, has_side_effects=True, vmem_limit_bytes=61 * 1024 * 1024),
        name="layer",
    )(
        queries,
        keys,
        values,
        residual,
        out_matrix.reshape(2, 8, width),
        norm_gain.reshape(1, width),
        block_mask,
        ids,
        gates,
        gate_matrix,
        lift_matrix,
        down_matrix,
    )


def shards(
    queries,
    encoded_key_heads,
    value_head_vectors,
    residual,
    out_matrix,
    norm_gain,
    expert_ids,
    expert_gates,
    gate_matrix,
    lift_matrix,
    down_matrix,
    block_mask,
):
    return layer(
        queries,
        encoded_key_heads,
        value_head_vectors,
        residual,
        out_matrix,
        norm_gain,
        block_mask,
        expert_ids.T,
        expert_gates.T,
        gate_matrix,
        lift_matrix,
        down_matrix,
    )


def solution(mesh):
    placed = (
        P(("rep", "ctx"), None),
        P(("rep", "ctx"), None),
        P(("rep", "ctx"), None),
        P(("rep", "ctx"), None),
        P("ctx", None),
        P(),
        P(("rep", "ctx"), None),
        P(("rep", "ctx"), None),
        P("ctx", None, None),
        P("ctx", None, None),
        P("ctx", None, None),
        P("rep", None),
    )
    return jax.shard_map(
        shards, mesh=mesh, in_specs=placed, out_specs=P(("rep", "ctx"), None), check_vma=False
    )
```

time: 294 us -> 199 us (0.68)
  starting transfers between devices: 65.2 us -> 0 us
  Pallas kernels: 134 us -> 196 us
  waiting for transfers between devices: 25.7 us -> 0 us
  matrix products: 21.6 us -> 0 us
  other arithmetic: 16.3 us -> 0 us
  local copies, waits for them, and re-layouts: 16.8 us -> 1.88 us
  between operations: 13.9 us -> 0.01 us
    ppermute x15 -> x0, starting transfers between devices: 65.2 us -> none  [shifted(): lax.ppermute(value, axis, [(source, source + steps) for source in range(i...]
    pallas_call x1, Pallas kernels: 134 us -> 196 us  [layer(): pl.pallas_call(layer_kernel, out_shape=jax.ShapeDtypeStruct((rows, width)...]
    all_gather x1 -> x0, waiting for transfers between devices: 22.2 us -> none  [shards(): lax.all_gather(out_matrix, 'ctx', axis=0, tiled=True)]
    sub x2 -> x0, matrix products: 11.5 us -> none  [attend(): weights = jnp.exp(scores - peak)]
    dot_general x3 -> x0, matrix products: 10.1 us -> none  [the longest x2 5.28 us: attend(): jnp.einsum('gtk,kd->tgd', probabilities, value_flattened[:, group_of_head...]
    unnamed x39 -> x1, local copies, waits for them, and re-layouts: 11.3 us -> 1.88 us
    lt x1 -> x0, other arithmetic: 5.57 us -> none  [attend(): shard_of[None, :] < block_extent - 1]
    gather x10 -> x0, other arithmetic: 4.83 us -> none  [attend(): open_key = jnp.take(shard_open, shard_of)]
  transfers between devices with their start and end apart: 16 -> 0, of which waited for: 2 -> 0; matrix products, arithmetic and copies ran while one was open for 15% -> 0% of each run, Pallas kernels for 0% -> 0%
where the time goes in v3:
time: 199 us; the launch traced here: 198 us
  Pallas kernels  196 us (98%)
    pallas_call x1, Pallas kernels, layer(): pl.pallas_call(layer_kernel, out_shape=jax.ShapeDtypeStruct((rows, width)...  196 us

profile of v3, /device:TPU:8, one launch (start us, length us, event | category | flops | bytes accessed | tf_op | source)
XLA Modules:
  0.0 198.4 jit_solution(18378758034242227927)
XLA Ops:
  0.0 196.5 %layer.1 = bf16[128,2048]{1,0:T(8,128)(2,1)} custom-call(bf16[128,2048]{1,0:T(8,128)(2,1)} %q_ref.1, bf16[128,256]{1,0:T(8,128)(2,1)} %k_ref.1, bf16[128,256]{1,0:T(8,128)(2,1)} %v_ref.1, bf16[128,2048]{1,0:T(8,128)(2,1)} %r_ref.1, bf16[2,8,2048]{2,1,0:T(8,128)(2,1)} %bitcast.4, f32[1,2048]{1,0:T(1,128)} %bitcast.5, s32[32,32]{1,0:T(8,128)} %b_ref.1, ...), custom_call_target="tpu_custom_call" | custom-call | tf_op jit(solution)/shard_map/layer/pallas_call | solution.py:531
  196.5 1.9 copy.14

commit v4 on v3

--- a/solution.py
+++ b/solution.py
@@ -21,7 +21,7 @@
 NX, NY, NZ = 4, 4, 8
 NQ = NX * NY
 NEG = -1e30
-COPIES = 112
+COPIES = 92
 
 
 def layer_kernel(
@@ -38,8 +38,7 @@
     wl_hbm,
     wd_hbm,
     o_ref,
-    kbuf,
-    vbuf,
+    kv,
     wfull,
     bias,
     s_ref,
@@ -125,13 +124,17 @@
 
     order = (1, 3, 2)
     z_order = (1, 7, 2, 6, 3, 5, 4)
-    part_c, part_a = 3 * width // 8, 5 * width // 16
-    pc, pa, pb = pl.ds(0, part_c), pl.ds(part_c, part_a), pl.ds(part_c + part_a, part_a)
+    part_c = 7 * width // 16
+    pc, pb = pl.ds(0, part_c), pl.ds(part_c, width - part_c)
+
+    def along_y(src, dst, d):
+        return send(src, dst, at(0, 0, 1 if d == 0 else NY - 1))
 
     c_x = [send(w_ref.at[r, :, pc], wfull.at[z, x, y, r, :, pc], at(0, d, 0)) for d in order]
-    k_next = {j: send(k_ref, kbuf.at[j, y], later(j)) for j in range(1, DOCUMENT_BLOCKS)}
-    v_row = [send(v_ref, vbuf.at[0, y], at(0, 0, d)) for d in order]
-    a_z = [send(w_ref.at[r, :, pa], wfull.at[z, x, y, r, :, pa], at(d, 0, 0)) for d in z_order]
+    nexts = {
+        j: [send(ref, kv.at[j, y, i], later(j)) for i, ref in enumerate((k_ref, v_ref))] for j in range(1, DOCUMENT_BLOCKS)
+    }
+    rows_of = {(0, d): [along_y(ref, kv.at[0, y, i], d) for i, ref in enumerate((k_ref, v_ref))] for d in range(2)}
     b_z = [send(w_ref.at[r, :, pb], wfull.at[z, x, y, r, :, pb], at(d, 0, 0)) for d in z_order]
     slot_of = {1: 1, 7: 2, 2: 3, 6: 4, 3: 5, 5: 6, 4: 7}
     tables = []
@@ -140,8 +143,8 @@
         tables.append(send(t_ref, gates.at[slot_of[d]], at(d, 0, 0)))
     ids[0] = i_ref[...]
     gates[0] = t_ref[...]
-    kbuf[0, y] = k_ref[...]
-    vbuf[0, y] = v_ref[...]
+    kv[0, y, 0] = k_ref[...]
+    kv[0, y, 1] = v_ref[...]
     wfull[z, x, y, r] = w_ref[r]
     shared = []
 
@@ -150,12 +153,17 @@
 
     landed(c_x)
     c_y = [send(wfull.at[z, :, y, r, :, pc], wfull.at[z, :, y, r, :, pc], at(0, 0, d)) for d in order]
-    k_row = [send(k_ref, kbuf.at[0, y], at(0, 0, d)) for d in order]
     for j in range(1, DOCUMENT_BLOCKS):
-        k_next[j].wait_recv()
-        k_row += [send(kbuf.at[j, y], kbuf.at[j, y], at(0, 0, d)) for d in order]
-    landed(v_row)
-    v_next = [send(vbuf.at[0], vbuf.at[j], later(j)) for j in range(1, DOCUMENT_BLOCKS)]
+        landed(nexts[j])
+        for d in range(2):
+            rows_of[j, d] = [along_y(kv.at[j, y], kv.at[j, y], d)]
+    relayed = []
+
+    def relay(j):
+        for d in range(2):
+            landed(rows_of[j, d])
+            came = lax.rem(y + (NY - 1 if d == 0 else 1), NY)
+            relayed.append(along_y(kv.at[j, came, d], kv.at[j, came, d], d))
 
     def plane(k, d):
         return lax.rem(z + (NZ - k if d == 0 else k), NZ)
@@ -181,13 +189,11 @@
                 c_z[d, e] = ring(k, d, e)
             share(ring_piece(k, d, e))
 
-    landed(a_z)
-    a_x = [send(wfull.at[:, x, y, r, :, pa], wfull.at[:, x, y, r, :, pa], at(0, d, 0)) for d in order]
+    relay(0)
     landed(b_z)
     b_y = [send(wfull.at[:, x, y, r, :, pb], wfull.at[:, x, y, r, :, pb], at(0, 0, d)) for d in order]
-
-    def last_a(i, zs):
-        return wfull.at[zs, :, i, r, :, pa]
+    for j in range(1, DOCUMENT_BLOCKS):
+        relay(j)
 
     def last_b(i, zs):
         return wfull.at[zs, i, :, r, :, pb]
@@ -197,7 +203,7 @@
     def step(of, i, d, zs):
         piece = of(i, zs)
         shift = 1 if d == 0 else NY - 1
-        return send(piece, piece, at(0, 0, shift) if of is last_a else at(0, shift, 0))
+        return send(piece, piece, at(0, shift, 0))
 
     def begin(of, i):
         share(of(i, every))
@@ -229,11 +235,9 @@
         bias[:, other * tokens : (other + 1) * tokens] = jnp.where(cols <= rows, 0.0, NEG)
 
 
-    landed(a_x)
-    a_last = begin(last_a, y)
+    forward(1)
     landed(b_y)
     b_last = begin(last_b, x)
-    forward(1)
     landed(tables)
     tri = (
         lax.broadcasted_iota(jnp.int32, (tokens, tokens), 0) < lax.broadcasted_iota(jnp.int32, (tokens, tokens), 1)
@@ -257,8 +261,7 @@
         return carry
 
     lax.fori_loop(0, NZ, all_keys, 0)
-    landed(k_row)
-    landed(v_next)
+    landed(relayed)
     forward(2)
 
     factor = math.log2(math.e) / math.sqrt(HEAD_SIZE)
@@ -270,7 +273,7 @@
         one = pl.ds(first, HEAD_SIZE)
         two = pl.ds(first + HEAD_SIZE, HEAD_SIZE)
         both = jnp.concatenate([q_ref[:, one], q_ref[:, two]], axis=0)
-        kk = kbuf[:, :, :, group].reshape(keys_all, HEAD_SIZE)
+        kk = kv[:, :, 0, :, group].reshape(keys_all, HEAD_SIZE)
         s_ref[...] = lax.dot_general(both, kk, (((1,), (1,)), ((), ())), preferred_element_type=f32)
 
         def soft(i, inner):
@@ -283,19 +286,17 @@
             return inner
 
         lax.fori_loop(0, 16, soft, 0, unroll=8)
-        vv = vbuf[:, :, :, group].reshape(keys_all, HEAD_SIZE)
+        vv = kv[:, :, 1, :, group].reshape(keys_all, HEAD_SIZE)
         o = jnp.dot(p_ref[...], vv, preferred_element_type=f32) / l_ref[...]
         att[:, one] = o[:tokens].astype(bf16)
         att[:, two] = o[tokens:].astype(bf16)
         return carry
 
     lax.fori_loop(0, 2, heads, 0)
-    a_end = pass_on(last_a, y, a_last)
     b_end = pass_on(last_b, x, b_last)
     forward(3)
     lax.fori_loop(2, 5, heads, 0)
     forward(4)
-    finish(last_a, y, a_end)
     finish(last_b, x, b_end)
     lax.fori_loop(5, 8, heads, 0)
     landed(shared)
@@ -321,13 +322,15 @@
 
     lax.fori_loop(0, width // tile, norm, 0)
 
-    half = tokens // 2
+    halves = [pl.ds(h * (width // 2), width // 2) for h in range(2)]
+    others = pl.ds(0, NQ - 1)
 
     def zpeer(d):
         return lax.rem(z + d, NZ) * NQ + q
 
     def qpeer(i):
-        return lax.rem(x + PLANE[i][0], NX) * NY + lax.rem(y + PLANE[i][1], NY)
+        a, b = PLANE[i]
+        return lax.rem(x + a + (b - a + NX) * r, NX) * NY + lax.rem(y + b + (a - b + NX) * r, NY)
 
     def remote(src, dst, s_sem, r_sem, dev):
         return pltpu.make_async_remote_copy(
@@ -336,9 +339,9 @@
 
     def zcopy(d, k, h):
         src = xg.at[0] if k == 0 else xg.at[2 * k - 1 + d]
-        rows = pl.ds(h * half, half)
         dst = xg.at[2 * k + 1 + d] if k < 3 else xg.at[7]
-        return remote(src.at[rows], dst.at[rows], zs.at[d, k, h], zr.at[d, k, h], zpeer(1 if d == 0 else NZ - 1))
+        cols = halves[h]
+        return remote(src.at[:, cols], dst.at[:, cols], zs.at[d, k, h], zr.at[d, k, h], zpeer(1 if d == 0 else NZ - 1))
 
     def zparts(k):
         return [(d, h) for h in range(2) for d in range(2) if k < 3 or d == h]
@@ -346,6 +349,7 @@
     for d, h in zparts(0):
         zcopy(d, 0, h).start()
     row = lax.broadcasted_iota(jnp.int32, (NQ, 8, tokens), 1)
+    chunk = width // 4
 
     def hits(b, first):
         return keys[b][:, None, :] == (row + first).astype(f32)
@@ -353,156 +357,162 @@
     def pick(b, first):
         return jnp.where(hits(b, first), 1.0, 0.0).reshape(NQ * 8, tokens).astype(bf16)
 
-    def build(t, blocks):
-        mats = [pick(b, first) for b, first in blocks]
-        chunk = width // 4
-
+    def blocks_of(t):
+        return [(b, 9 * (b == t - 1) - t) for b in (t - 1, t) if 0 <= b < NZ]
+
+    def fill(t, mats, h):
         def piece(c, carry):
             cols = pl.ds(pl.multiple_of(c * chunk, chunk), chunk)
             total = None
-            for (b, _), mat in zip(blocks, mats):
+            for (b, _), mat in zip(blocks_of(t), mats):
                 one = jnp.dot(mat, xg[b, :, cols], preferred_element_type=f32)
                 total = one if total is None else total + one
             outbox[t, :, :, cols] = total.astype(bf16).reshape(NQ, 8, chunk)
             return carry
 
-        lax.fori_loop(0, 4, piece, 0)
+        lax.fori_loop(2 * h, 2 * h + 2, piece, 0)
+
+    def exchange(src, dst, tiles, cols, s_sem, r_sem):
         for i in range(NQ - 1):
             p = qpeer(i)
-            remote(outbox.at[t, p], inbox.at[t, q], ds_.at[t], dr.at[t], z * NQ + p).start()
-        inbox[t, q] = outbox[t, q]
-
-    def dispatch(t):
-        if isinstance(t, int) and t == 0:
-            build(0, [(0, 0)])
-        elif isinstance(t, int) and t == 8:
-            build(8, [(7, 1)])
-        else:
-            build(t, [(t - 1, 9 - t), (t, -t)])
-
-    def wait_all(buf, sem):
-        pltpu.make_async_copy(buf, buf, sem).wait()
-
-    def mlp(first, count):
-        rows = count * NQ * 8
+            remote(src.at[tiles, p, :, cols], dst.at[tiles, q, :, cols], s_sem, r_sem, z * NQ + p).start()
+        dst[tiles, q, :, cols] = src[tiles, q, :, cols]
+
+    def piece_of(k, h):
+        return (pl.ds(0, 1), pl.ds(0, width), 0) if k < 0 else (pl.ds(2 * k + 1, 2), halves[h], 1 + 2 * k + h)
+
+    def dispatch(k, h):
+        tiles, cols, n = piece_of(k, h)
+        exchange(outbox, inbox, tiles, cols, ds_.at[n], dr.at[n])
+
+    def give_back(k, h):
+        tiles, cols, n = piece_of(k, h)
+        exchange(inbox, ret, tiles, cols, bs.at[n], br.at[n])
+
+    def all_of(buf, sem, k, h):
+        tiles, cols, n = piece_of(k, h)
+        part_of = buf.at[tiles, others, :, cols]
+        pltpu.make_async_copy(part_of, part_of, sem.at[n]).wait()
+
+    pieces = [(-1, 0)] + [(k, h) for k in range(4) for h in range(2)]
+
+    def mlp(first, count, finish_half):
+        rows = pl.ds(0, count * NQ * 8)
 
         def take(t, carry):
-            wait_all(inbox.at[first + t, pl.ds(0, NQ - 1)], dr.at[first + t])
             xs[pl.ds(pl.multiple_of(t * NQ * 8, NQ * 8), NQ * 8), :] = inbox[first + t].reshape(NQ * 8, width)
             return carry
 
         lax.fori_loop(0, count, take, 0)
-        hidden = wg.shape[1]
-        tile = 256
 
         def up(c, carry):
             cols = pl.ds(pl.multiple_of(c * tile, tile), tile)
-            g = jnp.dot(xs[pl.ds(0, rows), :], wg[:, cols], preferred_element_type=f32)
-            u = jnp.dot(xs[pl.ds(0, rows), :], wl[:, cols], preferred_element_type=f32)
-            act[pl.ds(0, rows), cols] = (g / (1.0 + jnp.exp(-g)) * u).astype(bf16)
+            g = jnp.dot(xs[rows, :], wg[:, cols], preferred_element_type=f32)
+            u = jnp.dot(xs[rows, :], wl[:, cols], preferred_element_type=f32)
+            act[rows, cols] = (g / (1.0 + jnp.exp(-g)) * u).astype(bf16)
             return carry
 
-        lax.fori_loop(0, hidden // tile, up, 0)
+        lax.fori_loop(0, wg.shape[1] // tile, up, 0)
 
         def down(c, carry):
             cols = pl.ds(pl.multiple_of(c * tile, tile), tile)
-            y = jnp.dot(act[pl.ds(0, rows), :], wd[:, cols], preferred_element_type=f32)
-            inbox[pl.ds(first, count), :, :, cols] = y.astype(bf16).reshape(count, NQ, 8, tile)
+            out = jnp.dot(act[rows, :], wd[:, cols], preferred_element_type=f32)
+            inbox[pl.ds(first, count), :, :, cols] = out.astype(bf16).reshape(count, NQ, 8, tile)
             return carry
 
-        lax.fori_loop(0, width // tile, down, 0)
-
-    def give_back(t):
-        for i in range(NQ - 1):
-            p = qpeer(i)
-            remote(inbox.at[t, p], ret.at[t, q], bs.at[t], br.at[t], z * NQ + p).start()
-        ret[t, q] = inbox[t, q]
-
-    dispatch(0)
-    groups = ((0, 3), (3, 2), (5, 2), (7, 2))
+        steps = width // tile
+        for h in range(2):
+            lax.fori_loop(h * steps // 2, (h + 1) * steps // 2, down, 0)
+            finish_half(h)
+
+    for h in range(2):
+        fill(0, [pick(*b) for b in blocks_of(0)], h)
+    dispatch(-1, 0)
     for k in range(4):
-        for d, h in zparts(k):
-            zcopy(d, k, h).wait_recv()
-            if k < 3 and (d, h) in zparts(k + 1):
-                zcopy(d, k + 1, h).start()
-        if k < 3:
-
-            def two(t, carry):
-                dispatch(t)
-                return carry
-
-            lax.fori_loop(2 * k + 1, 2 * k + 3, two, 0)
-        else:
-            dispatch(7)
-            dispatch(8)
+        mats = [[pick(*b) for b in blocks_of(t)] for t in (2 * k + 1, 2 * k + 2)]
+        for h in range(2):
+            for d in range(2):
+                if (d, h) in zparts(k):
+                    zcopy(d, k, h).wait_recv()
+                    if k < 3 and (d, h) in zparts(k + 1):
+                        zcopy(d, k + 1, h).start()
+            for t, mat in zip((2 * k + 1, 2 * k + 2), mats):
+                fill(t, mat, h)
+            dispatch(k, h)
         if k == 0:
             for c in weights:
                 c.wait()
+            all_of(inbox, dr, -1, 0)
         else:
-            mlp(*groups[k - 1])
-    mlp(*groups[3])
-
-    def back(t, carry):
-        give_back(8 - t)
-        return carry
-
-    lax.fori_loop(0, 9, back, 0)
-
-    def wait_ret(t):
-        wait_all(ret.at[t, pl.ds(0, NQ - 1)], br.at[t])
-
-    def partial(b, slot):
+            all_of(inbox, dr, k - 1, 0)
+            all_of(inbox, dr, k - 1, 1)
+            mlp(2 * k - 1 if k > 1 else 0, 2 if k > 1 else 3, lambda h: None)
+    all_of(inbox, dr, 3, 0)
+    all_of(inbox, dr, 3, 1)
+    mlp(7, 2, lambda h: give_back(3, h))
+    for k in (2, 1, 0):
+        for h in range(2):
+            give_back(k, h)
+    give_back(-1, 0)
+
+    def gated(b):
         lo = jnp.where(hits(b, -b), gts[b][:, None, :], 0.0).reshape(NQ * 8, tokens)
         hi = jnp.where(hits(b, 8 - b), gts[b][:, None, :], 0.0).reshape(NQ * 8, tokens)
-        mat = jnp.concatenate([lo, hi], axis=0).T.astype(bf16)
-        chunk = width // 4
-
+        return jnp.concatenate([lo, hi], axis=0).T.astype(bf16)
+
+    def partial(b, mat, slot, h):
         def piece(c, carry):
             cols = pl.ds(pl.multiple_of(c * chunk, chunk), chunk)
             rows = ret[b : b + 2, :, :, cols].reshape(2 * NQ * 8, chunk)
             part[slot, :, cols] = jnp.dot(mat, rows, preferred_element_type=f32)
             return carry
 
-        lax.fori_loop(0, 4, piece, 0)
+        lax.fori_loop(2 * h, 2 * h + 2, piece, 0)
 
     def scopy(d, k, h):
-        rows = pl.ds(h * half, half)
+        cols = halves[h]
         return remote(
-            rsend.at[d, k, rows], rrecv.at[d, k, rows], ss.at[d, k, h], sr.at[d, k, h], zpeer(1 if d == 0 else NZ - 1)
+            rsend.at[d, k, :, cols],
+            rrecv.at[d, k, :, cols],
+            ss.at[d, k, h],
+            sr.at[d, k, h],
+            zpeer(1 if d == 0 else NZ - 1),
         )
 
     def sparts(k):
         return [(d, h) for h in range(2) for d in range(2) if k > 0 or d == h]
 
-    wait_ret(8)
-    wait_ret(7)
-    partial(7, 0)
-    for d, h in sparts(0):
-        rows = pl.ds(h * half, half)
-        rsend[d, 0, rows] = part[0, rows].astype(bf16)
-        scopy(d, 0, h).start()
+    mat = gated(7)
+    for h in range(2):
+        cols = halves[h]
+        all_of(ret, br, 3, h)
+        partial(7, mat, 0, h)
+        rsend[h, 0, :, cols] = part[0, :, cols].astype(bf16)
+        scopy(h, 0, h).start()
     for k in range(1, 4):
-        wait_ret(8 - 2 * k)
-        wait_ret(7 - 2 * k)
-        partial(8 - 2 * k, 0)
-        partial(7 - 2 * k, 1)
-        for d, h in sparts(k):
-            rows = pl.ds(h * half, half)
-            total = part[d, rows]
-            if (d, h) in sparts(k - 1):
-                scopy(d, k - 1, h).wait_recv()
-                total = total + rrecv[d, k - 1, rows].astype(f32)
-            rsend[d, k, rows] = total.astype(bf16)
-            scopy(d, k, h).start()
-    wait_ret(0)
-    partial(0, 0)
+        mats = [gated(8 - 2 * k), gated(7 - 2 * k)]
+        for h in range(2):
+            cols = halves[h]
+            all_of(ret, br, 3 - k, h)
+            for d in range(2):
+                partial(8 - 2 * k - d, mats[d], d, h)
+            for d in range(2):
+                total = part[d, :, cols]
+                if (d, h) in sparts(k - 1):
+                    scopy(d, k - 1, h).wait_recv()
+                    total = total + rrecv[d, k - 1, :, cols].astype(f32)
+                rsend[d, k, :, cols] = total.astype(bf16)
+                scopy(d, k, h).start()
+    mat = gated(0)
+    all_of(ret, br, -1, 0)
     for h in range(2):
-        rows = pl.ds(h * half, half)
-        total = part[0, rows] + h_ref[rows, :].astype(f32)
+        cols = halves[h]
+        partial(0, mat, 0, h)
+        total = part[0, :, cols] + h_ref[:, cols].astype(f32)
         for d in range(2):
             scopy(d, 3, h).wait_recv()
-            total = total + rrecv[d, 3, rows].astype(f32)
-        o_ref[rows, :] = total.astype(bf16)
+            total = total + rrecv[d, 3, :, cols].astype(f32)
+        o_ref[:, cols] = total.astype(bf16)
 
     for c in copies:
         c.wait_send()
@@ -511,13 +521,9 @@
             zcopy(d, k, h).wait_send()
         for d, h in sparts(k):
             scopy(d, k, h).wait_send()
-
-    def sent(t, carry):
-        wait_all(outbox.at[t, pl.ds(0, NQ - 1)], ds_.at[t])
-        wait_all(inbox.at[t, pl.ds(0, NQ - 1)], bs.at[t])
-        return carry
-
-    lax.fori_loop(0, 9, sent, 0)
+    for k, h in pieces:
+        all_of(outbox, ds_, k, h)
+        all_of(inbox, bs, k, h)
 
 
 def layer(queries, keys, values, residual, out_matrix, norm_gain, block_mask, ids, gates, gate_matrix, lift_matrix, down_matrix):
@@ -534,8 +540,7 @@
         in_specs=[vmem] * 6 + [pl.BlockSpec(memory_space=pltpu.SMEM), vmem, vmem, hbm, hbm, hbm],
         out_specs=vmem,
         scratch_shapes=[
-            pltpu.VMEM((DOCUMENT_BLOCKS, NY, rows, group), bf16),
-            pltpu.VMEM((DOCUMENT_BLOCKS, NY, rows, group), bf16),
+            pltpu.VMEM((DOCUMENT_BLOCKS, NY, 2, rows, group), bf16),
             pltpu.VMEM((NZ, NX, NY, 2, 8, width), bf16),
             pltpu.VMEM((rows, reach), f32),
             pltpu.VMEM((2 * rows, reach), f32),

time: 199 us -> 189 us (0.950)
  Pallas kernels: 196 us -> 186 us
    pallas_call x1, Pallas kernels: 196 us -> 186 us  [layer(): pl.pallas_call(layer_kernel, out_shape=jax.ShapeDtypeStruct((rows, width)...]
where the time goes in v4:
time: 189 us; the launch traced here: 188 us
  Pallas kernels  186 us (98%)
    pallas_call x1, Pallas kernels, layer(): pl.pallas_call(layer_kernel, out_shape=jax.ShapeDtypeStruct((rows, width)...  186 us

profile of v4, /device:TPU:8, one launch (start us, length us, event | category | flops | bytes accessed | tf_op | source)
XLA Modules:
  0.0 188.3 jit_solution(11579331965442350434)
XLA Ops:
  0.0 186.4 %layer.1 = bf16[128,2048]{1,0:T(8,128)(2,1)} custom-call(bf16[128,2048]{1,0:T(8,128)(2,1)} %q_ref.1, bf16[128,256]{1,0:T(8,128)(2,1)} %k_ref.1, bf16[128,256]{1,0:T(8,128)(2,1)} %v_ref.1, bf16[128,2048]{1,0:T(8,128)(2,1)} %r_ref.1, bf16[2,8,2048]{2,1,0:T(8,128)(2,1)} %bitcast.4, f32[1,2048]{1,0:T(1,128)} %bitcast.5, s32[32,32]{1,0:T(8,128)} %b_ref.1, ...), custom_call_target="tpu_custom_call" | custom-call | tf_op jit(solution)/shard_map/layer/pallas_call | solution.py:537
  186.4 1.9 copy.14
